TPU v7x, 768 devices: a whole 4x8x12 slice. The times are simulated.
768 devices in a mesh: grp: 4 (over x_hi, core), row: 8 (over y), col: 24 (over z, x_lo).
Axes of the slice: x: 4 (x_hi: 2, x_lo: 2; x = x_hi * 2 + x_lo), y: 8, z: 12, core: 2. Of those that a mesh axis runs over, the one named last changes fastest.
Arguments:
- velocity: float32 [3, 24, 1024, 1024], P(None, 'col', ('grp', 'row')), may hold values from -8 to 8
- profile: int32 [24], P('col'), may hold values from 0 to 1
- x_filters: bfloat16 [2, 1024, 1024], replicated, may hold values from 0 to 1
- z_filter: bfloat16 [1024, 1024], replicated, may hold values from 0 to 1
Outputs:
- stress: float32 [6, 24, 1024, 1024], P(None, 'col', ('grp', 'row'))
All inputs are finite; a program needn't handle non-finite values.
Results may differ from a plain program's by a relative error of at most 0.0031.
Values may be sent and summed in bfloat16 or wider, within the bound.
A program may use at most 32 MiB of HBM per device.

v0:
```python
import jax
import jax.numpy as jnp
from jax import lax
from jax.sharding import PartitionSpec as P

STEP_SIZE = 0.25
VISCOSITY = 0.8
PRODUCT_PAIRS = ((0, 0), (0, 1), (0, 2), (1, 1), (1, 2), (2, 2))


def extended(cells, sides, width):
    for axis, dim in sides:
        count = lax.axis_size(axis)
        head = lax.slice_in_dim(cells, 0, width, axis=dim)
        tail = lax.slice_in_dim(cells, cells.shape[dim] - width, cells.shape[dim], axis=dim)
        cells = jnp.concatenate(
            [
                lax.ppermute(tail, axis, [(i, (i + 1) % count) for i in range(count)]),
                cells,
                lax.ppermute(head, axis, [((i + 1) % count, i) for i in range(count)]),
            ],
            axis=dim,
        )
    return cells


def wall_zero(padded, extent, y_rows):
    height = padded.shape[1]
    all_rows = y_rows * lax.axis_size("col")
    row_index = lax.axis_index("col") * y_rows + jnp.arange(height, dtype=jnp.int32) - extent
    inside = (row_index >= 0) & (row_index < all_rows)
    return padded * inside.astype(padded.dtype)[None, :, None, None]


def shrink_rate(padded):
    center = padded[:, 1:-1, 1:-1]
    y_next = padded[:, 2:, 1:-1]
    y_prev = padded[:, :-2, 1:-1]
    z_next = padded[:, 1:-1, 2:]
    z_prev = padded[:, 1:-1, :-2]
    x_next = jnp.roll(center, -1, axis=3)
    x_prev = jnp.roll(center, 1, axis=3)
    advect = (
        center[0] * (0.5 * (x_next - x_prev))
        + center[1] * (0.5 * (y_next - y_prev))
        + center[2] * (0.5 * (z_next - z_prev))
    )
    laplace = x_next + x_prev + y_next + y_prev + z_next + z_prev - 6.0 * center
    return VISCOSITY * laplace - advect


def z_apply(received, z_filter):
    return jnp.einsum("fyos,rs->fyor", received, z_filter, preferred_element_type=jnp.float32)


def body(velocity, profile, x_filters, z_filter):
    y_rows = velocity.shape[1]

    def extend(current):
        padded = extended(current, ((("grp", "row"), 2), ("col", 1)), 1)
        return wall_zero(padded, 1, y_rows)

    section_one = velocity + STEP_SIZE * shrink_rate(extend(velocity))
    section_two = 0.75 * velocity + 0.25 * (
        section_one + STEP_SIZE * shrink_rate(extend(section_one))
    )
    advanced = velocity / 3.0 + 2.0 / 3.0 * (
        section_two + STEP_SIZE * shrink_rate(extend(section_two))
    )
    components = [advanced[0], advanced[1], advanced[2]] + [
        advanced[left_comp] * advanced[right_comp] for left_comp, right_comp in PRODUCT_PAIRS
    ]
    fields = jnp.stack(components).astype(jnp.bfloat16)
    matrices = jnp.take(x_filters, profile, axis=0)
    x_pass = jnp.einsum(
        "yox,fyzx->fyoz", matrices, fields, preferred_element_type=jnp.float32
    ).astype(jnp.bfloat16)
    filtered = z_apply(
        lax.all_to_all(x_pass, ("grp", "row"), split_axis=2, concat_axis=3, tiled=True), z_filter
    )
    stress = jnp.stack(
        [
            filtered[3 + number] - filtered[left_comp] * filtered[right_comp]
            for number, (left_comp, right_comp) in enumerate(PRODUCT_PAIRS)
        ]
    )
    return stress


def solution(mesh):
    placed = (P(None, "col", ("grp", "row"), None), P("col"), P(), P())
    return jax.shard_map(
        body,
        mesh=mesh,
        in_specs=placed,
        out_specs=P(None, "col", ("grp", "row"), None),
        check_vma=False,
    )
```

profile of v0, /device:TPU:1, one launch (start us, length us, event | category | flops | bytes accessed | tf_op | source)
XLA Modules:
  0.0 179.8 jit_solution(18378187300313996776)
XLA Ops:
  1.1 4.0 %collective-permute-start = (f32[3,1,1,1024]{3,2,1,0:T(1,128)S(1)}, f32[3,1,1,1024]{3,2,1,0:T(1,128)S(1)}, u32[]{:S(2)}, u32[]{:S(2)}) collective-permute-start(f32[3,1,1,1024]{3,2,1,0:T(1,128)S(1)} %get-tuple-element.43), channel_id=1, source_target_pairs={{0,24},{24,48},{48,72},{72,96},{96,120},{120,144},{144,168},{168,1... | collective-permute-start | bytes 36872 | tf_op jit(solution)/shard_map/ppermute | solution.py:18
  5.2 4.4 %collective-permute-start.1 = (f32[3,1,1,1024]{3,2,1,0:T(1,128)S(1)}, f32[3,1,1,1024]{3,2,1,0:T(1,128)S(1)}, u32[]{:S(2)}, u32[]{:S(2)}) collective-permute-start(f32[3,1,1,1024]{3,2,1,0:T(1,128)S(1)} %get-tuple-element.44), channel_id=1, source_target_pairs={{24,0},{48,24},{72,48},{96,72},{120,96},{144,120},{168,144},{192,1... | collective-permute-start | bytes 36872 | tf_op jit(solution)/shard_map/ppermute | solution.py:20
  12.2 15.2 %collective-permute-start.3 = (f32[3,1,34,1024]{3,2,1,0:T(8,128)}, f32[3,1,34,1024]{3,2,1,0:T(8,128)S(1)}, u32[]{:S(2)}, u32[]{:S(2)}) collective-permute-start(f32[3,1,34,1024]{3,2,1,0:T(8,128)} %pad_maximum_fusion), channel_id=1, source_target_pairs={{1,0},{2,1},{3,2},{4,3},{5,4},{6,5},{7,6},{8,7},{9,8},{10,9},{11,1... | collective-permute-start | bytes 1253384 | tf_op jit(solution)/shard_map/ppermute | solution.py:20
  27.4 1.9 %collective-permute-start.2 = (f32[3,1,34,1024]{3,2,1,0:T(8,128)}, f32[3,1,34,1024]{3,2,1,0:T(8,128)S(1)}, u32[]{:S(2)}, u32[]{:S(2)}) collective-permute-start(f32[3,1,34,1024]{3,2,1,0:T(8,128)} %pad_maximum_fusion), channel_id=1, source_target_pairs={{0,1},{1,2},{2,3},{3,4},{4,5},{5,6},{6,7},{7,8},{8,9},{9,10},{10,1... | collective-permute-start | bytes 1253384 | tf_op jit(solution)/shard_map/ppermute | solution.py:18
  29.4 6.1 %collective-permute-done.3 = f32[3,1,34,1024]{3,2,1,0:T(8,128)S(1)} collective-permute-done((f32[3,1,34,1024]{3,2,1,0:T(8,128)}, f32[3,1,34,1024]{3,2,1,0:T(8,128)S(1)}, u32[]{:S(2)}, u32[]{:S(2)}) %collective-permute-start.3) | collective-permute-done | bytes 417824 | tf_op jit(solution)/shard_map/ppermute | solution.py:20
  35.5 5.8 %collective-permute-done.2 = f32[3,1,34,1024]{3,2,1,0:T(8,128)S(1)} collective-permute-done((f32[3,1,34,1024]{3,2,1,0:T(8,128)}, f32[3,1,34,1024]{3,2,1,0:T(8,128)S(1)}, u32[]{:S(2)}, u32[]{:S(2)}) %collective-permute-start.2) | collective-permute-done | bytes 417824 | tf_op jit(solution)/shard_map/ppermute | solution.py:18
  44.0 3.1 %collective-permute-start.4 = (f32[3,1,1,1024]{3,2,1,0:T(1,128)S(1)}, f32[3,1,1,1024]{3,2,1,0:T(1,128)S(1)}, u32[]{:S(2)}, u32[]{:S(2)}) collective-permute-start(f32[3,1,1,1024]{3,2,1,0:T(1,128)S(1)} %get-tuple-element.41), channel_id=1, source_target_pairs={{0,24},{24,48},{48,72},{72,96},{96,120},{120,144},{144,168},{168,1... | collective-permute-start | bytes 36872 | tf_op jit(solution)/shard_map/ppermute | solution.py:18
  47.2 6.3 %collective-permute-start.5 = (f32[3,1,1,1024]{3,2,1,0:T(1,128)S(1)}, f32[3,1,1,1024]{3,2,1,0:T(1,128)S(1)}, u32[]{:S(2)}, u32[]{:S(2)}) collective-permute-start(f32[3,1,1,1024]{3,2,1,0:T(1,128)S(1)} %get-tuple-element.42), channel_id=1, source_target_pairs={{24,0},{48,24},{72,48},{96,72},{120,96},{144,120},{168,144},{192,1... | collective-permute-start | bytes 36872 | tf_op jit(solution)/shard_map/ppermute | solution.py:20
  54.3 12.8 %collective-permute-start.7 = (f32[3,1,34,1024]{3,2,1,0:T(8,128)S(1)}, f32[3,1,34,1024]{3,2,1,0:T(8,128)S(1)}, u32[]{:S(2)}, u32[]{:S(2)}) collective-permute-start(f32[3,1,34,1024]{3,2,1,0:T(8,128)S(1)} %pad_maximum_fusion.1), channel_id=1, source_target_pairs={{1,0},{2,1},{3,2},{4,3},{5,4},{6,5},{7,6},{8,7},{9,8},{10,9},{11,1... | collective-permute-start | bytes 1253384 | tf_op jit(solution)/shard_map/ppermute | solution.py:20
  67.1 1.9 %collective-permute-start.6 = (f32[3,1,34,1024]{3,2,1,0:T(8,128)S(1)}, f32[3,1,34,1024]{3,2,1,0:T(8,128)S(1)}, u32[]{:S(2)}, u32[]{:S(2)}) collective-permute-start(f32[3,1,34,1024]{3,2,1,0:T(8,128)S(1)} %pad_maximum_fusion.1), channel_id=1, source_target_pairs={{0,1},{1,2},{2,3},{3,4},{4,5},{5,6},{6,7},{7,8},{8,9},{9,10},{10,1... | collective-permute-start | bytes 1253384 | tf_op jit(solution)/shard_map/ppermute | solution.py:18
  69.1 6.4 %collective-permute-done.7 = f32[3,1,34,1024]{3,2,1,0:T(8,128)S(1)} collective-permute-done((f32[3,1,34,1024]{3,2,1,0:T(8,128)S(1)}, f32[3,1,34,1024]{3,2,1,0:T(8,128)S(1)}, u32[]{:S(2)}, u32[]{:S(2)}) %collective-permute-start.7) | collective-permute-done | bytes 417824 | tf_op jit(solution)/shard_map/ppermute | solution.py:20
  75.5 5.9 %collective-permute-done.6 = f32[3,1,34,1024]{3,2,1,0:T(8,128)S(1)} collective-permute-done((f32[3,1,34,1024]{3,2,1,0:T(8,128)S(1)}, f32[3,1,34,1024]{3,2,1,0:T(8,128)S(1)}, u32[]{:S(2)}, u32[]{:S(2)}) %collective-permute-start.6) | collective-permute-done | bytes 417824 | tf_op jit(solution)/shard_map/ppermute | solution.py:18
  82.4 4.0 %collective-permute-start.8 = (f32[3,1,1,1024]{3,2,1,0:T(1,128)S(1)}, f32[3,1,1,1024]{3,2,1,0:T(1,128)S(1)}, u32[]{:S(2)}, u32[]{:S(2)}) collective-permute-start(f32[3,1,1,1024]{3,2,1,0:T(1,128)S(1)} %get-tuple-element.39), channel_id=1, source_target_pairs={{0,24},{24,48},{48,72},{72,96},{96,120},{120,144},{144,168},{168,1... | collective-permute-start | bytes 36872 | tf_op jit(solution)/shard_map/ppermute | solution.py:18
  86.4 5.7 %collective-permute-start.9 = (f32[3,1,1,1024]{3,2,1,0:T(1,128)S(1)}, f32[3,1,1,1024]{3,2,1,0:T(1,128)S(1)}, u32[]{:S(2)}, u32[]{:S(2)}) collective-permute-start(f32[3,1,1,1024]{3,2,1,0:T(1,128)S(1)} %get-tuple-element.40), channel_id=1, source_target_pairs={{24,0},{48,24},{72,48},{96,72},{120,96},{144,120},{168,144},{192,1... | collective-permute-start | bytes 36872 | tf_op jit(solution)/shard_map/ppermute | solution.py:20
  93.0 11.6 %collective-permute-start.11 = (f32[3,1,34,1024]{3,2,1,0:T(8,128)S(1)}, f32[3,1,34,1024]{3,2,1,0:T(8,128)S(1)}, u32[]{:S(2)}, u32[]{:S(2)}) collective-permute-start(f32[3,1,34,1024]{3,2,1,0:T(8,128)S(1)} %pad_maximum_fusion.2), channel_id=1, source_target_pairs={{1,0},{2,1},{3,2},{4,3},{5,4},{6,5},{7,6},{8,7},{9,8},{10,9},{11,1... | collective-permute-start | bytes 1253384 | tf_op jit(solution)/shard_map/ppermute | solution.py:20
  104.6 1.9 %collective-permute-start.10 = (f32[3,1,34,1024]{3,2,1,0:T(8,128)S(1)}, f32[3,1,34,1024]{3,2,1,0:T(8,128)S(1)}, u32[]{:S(2)}, u32[]{:S(2)}) collective-permute-start(f32[3,1,34,1024]{3,2,1,0:T(8,128)S(1)} %pad_maximum_fusion.2), channel_id=1, source_target_pairs={{0,1},{1,2},{2,3},{3,4},{4,5},{5,6},{6,7},{7,8},{8,9},{9,10},{10,1... | collective-permute-start | bytes 1253384 | tf_op jit(solution)/shard_map/ppermute | solution.py:18
  107.2 5.7 %collective-permute-done.11 = f32[3,1,34,1024]{3,2,1,0:T(8,128)S(1)} collective-permute-done((f32[3,1,34,1024]{3,2,1,0:T(8,128)S(1)}, f32[3,1,34,1024]{3,2,1,0:T(8,128)S(1)}, u32[]{:S(2)}, u32[]{:S(2)}) %collective-permute-start.11) | collective-permute-done | bytes 417824 | tf_op jit(solution)/shard_map/ppermute | solution.py:20
  113.0 5.9 %collective-permute-done.10 = f32[3,1,34,1024]{3,2,1,0:T(8,128)S(1)} collective-permute-done((f32[3,1,34,1024]{3,2,1,0:T(8,128)S(1)}, f32[3,1,34,1024]{3,2,1,0:T(8,128)S(1)}, u32[]{:S(2)}, u32[]{:S(2)}) %collective-permute-start.10) | collective-permute-done | bytes 417824 | tf_op jit(solution)/shard_map/ppermute | solution.py:18
  122.4 4.7 %copy.6 = bf16[9,1,1024,32]{3,0,1,2:T(8,128)(2,1)} copy(bf16[9,1,1024,32]{2,3,0,1:T(8,128)(2,1)S(1)} %fusion.8) | data formatting | bytes 1179648 | tf_op jit(solution)/shard_map/convert_element_type | solution.py:77
  127.2 5.3 %reshape.503 = bf16[32,2,4608]{2,1,0:T(2,128)(2,1)S(1)} reshape(bf16[1024,1,9,32]{3,2,1,0:T(8,128)(2,1)} %bitcast.97) | data formatting | bytes 1179648
  132.5 29.9 %all_to_all.15 = bf16[32,2,4608]{2,1,0:T(2,128)(2,1)} all-to-all(bf16[32,2,4608]{2,1,0:T(2,128)(2,1)S(1)} %reshape.503), channel_id=1, replica_groups=mesh['grp'=4,'row'=8,'col'=24] {'grp','row'}, dimensions={0} | all-to-all | bytes 1179648 | tf_op jit(solution)/shard_map/all_to_all | solution.py:79
  162.4 5.8 %reshape.504 = bf16[1024,1,9,32]{3,2,1,0:T(8,128)(2,1)} reshape(bf16[32,2,4608]{2,1,0:T(2,128)(2,1)} %all_to_all.15) | data formatting | bytes 1179648
  168.1 5.3 %copy.9 = bf16[9,1,32,32,32]{4,2,3,0,1:T(8,128)(2,1)} copy(bf16[9,1,32,32,32]{4,0,3,2,1:T(8,128)(2,1)} %bitcast.98) | data formatting | bytes 1179648 | tf_op jit(solution)/shard_map/all_to_all | solution.py:79
  173.4 3.9 %reshape.472 = bf16[9,32,1024]{2,1,0:T(8,128)(2,1)S(1)} reshape(bf16[9,1,32,32,32]{4,3,2,0,1:T(8,128)(2,1)} %bitcast.99) | data formatting | bytes 1179648 | tf_op jit(solution)/shard_map/reshape.14
  (50 shorter events, 15.2 us)
Async XLA Ops:
  0.0 177.3 %copy-start = (bf16[1024,1024]{1,0:T(8,128)(2,1)S(1)}, bf16[1024,1024]{1,0:T(8,128)(2,1)}, u32[]{:S(2)}) copy-start(bf16[1024,1024]{1,0:T(8,128)(2,1)} %param.7) | copy-start | bytes 6291460
  1.1 8.4 %collective-permute-start = (f32[3,1,1,1024]{3,2,1,0:T(1,128)S(1)}, f32[3,1,1,1024]{3,2,1,0:T(1,128)S(1)}, u32[]{:S(2)}, u32[]{:S(2)}) collective-permute-start(f32[3,1,1,1024]{3,2,1,0:T(1,128)S(1)} %get-tuple-element.43), channel_id=1, source_target_pairs={{0,24},{24,48},{48,72},{72,96},{96,120},{120,144},{144,168},{168,1... | collective-permute-start | bytes 36872 | tf_op jit(solution)/shard_map/ppermute | solution.py:18
  5.2 5.2 %collective-permute-start.1 = (f32[3,1,1,1024]{3,2,1,0:T(1,128)S(1)}, f32[3,1,1,1024]{3,2,1,0:T(1,128)S(1)}, u32[]{:S(2)}, u32[]{:S(2)}) collective-permute-start(f32[3,1,1,1024]{3,2,1,0:T(1,128)S(1)} %get-tuple-element.44), channel_id=1, source_target_pairs={{24,0},{48,24},{72,48},{96,72},{120,96},{144,120},{168,144},{192,1... | collective-permute-start | bytes 36872 | tf_op jit(solution)/shard_map/ppermute | solution.py:20
  12.2 23.3 %collective-permute-start.3 = (f32[3,1,34,1024]{3,2,1,0:T(8,128)}, f32[3,1,34,1024]{3,2,1,0:T(8,128)S(1)}, u32[]{:S(2)}, u32[]{:S(2)}) collective-permute-start(f32[3,1,34,1024]{3,2,1,0:T(8,128)} %pad_maximum_fusion), channel_id=1, source_target_pairs={{1,0},{2,1},{3,2},{4,3},{5,4},{6,5},{7,6},{8,7},{9,8},{10,9},{11,1... | collective-permute-start | bytes 1253384 | tf_op jit(solution)/shard_map/ppermute | solution.py:20
  27.4 13.9 %collective-permute-start.2 = (f32[3,1,34,1024]{3,2,1,0:T(8,128)}, f32[3,1,34,1024]{3,2,1,0:T(8,128)S(1)}, u32[]{:S(2)}, u32[]{:S(2)}) collective-permute-start(f32[3,1,34,1024]{3,2,1,0:T(8,128)} %pad_maximum_fusion), channel_id=1, source_target_pairs={{0,1},{1,2},{2,3},{3,4},{4,5},{5,6},{6,7},{7,8},{8,9},{9,10},{10,1... | collective-permute-start | bytes 1253384 | tf_op jit(solution)/shard_map/ppermute | solution.py:18
  42.6 1.0 copy-start.1
  44.0 9.4 %collective-permute-start.4 = (f32[3,1,1,1024]{3,2,1,0:T(1,128)S(1)}, f32[3,1,1,1024]{3,2,1,0:T(1,128)S(1)}, u32[]{:S(2)}, u32[]{:S(2)}) collective-permute-start(f32[3,1,1,1024]{3,2,1,0:T(1,128)S(1)} %get-tuple-element.41), channel_id=1, source_target_pairs={{0,24},{24,48},{48,72},{72,96},{96,120},{120,144},{144,168},{168,1... | collective-permute-start | bytes 36872 | tf_op jit(solution)/shard_map/ppermute | solution.py:18
  47.2 7.1 %collective-permute-start.5 = (f32[3,1,1,1024]{3,2,1,0:T(1,128)S(1)}, f32[3,1,1,1024]{3,2,1,0:T(1,128)S(1)}, u32[]{:S(2)}, u32[]{:S(2)}) collective-permute-start(f32[3,1,1,1024]{3,2,1,0:T(1,128)S(1)} %get-tuple-element.42), channel_id=1, source_target_pairs={{24,0},{48,24},{72,48},{96,72},{120,96},{144,120},{168,144},{192,1... | collective-permute-start | bytes 36872 | tf_op jit(solution)/shard_map/ppermute | solution.py:20
  54.3 21.1 %collective-permute-start.7 = (f32[3,1,34,1024]{3,2,1,0:T(8,128)S(1)}, f32[3,1,34,1024]{3,2,1,0:T(8,128)S(1)}, u32[]{:S(2)}, u32[]{:S(2)}) collective-permute-start(f32[3,1,34,1024]{3,2,1,0:T(8,128)S(1)} %pad_maximum_fusion.1), channel_id=1, source_target_pairs={{1,0},{2,1},{3,2},{4,3},{5,4},{6,5},{7,6},{8,7},{9,8},{10,9},{11,1... | collective-permute-start | bytes 1253384 | tf_op jit(solution)/shard_map/ppermute | solution.py:20
  67.1 14.2 %collective-permute-start.6 = (f32[3,1,34,1024]{3,2,1,0:T(8,128)S(1)}, f32[3,1,34,1024]{3,2,1,0:T(8,128)S(1)}, u32[]{:S(2)}, u32[]{:S(2)}) collective-permute-start(f32[3,1,34,1024]{3,2,1,0:T(8,128)S(1)} %pad_maximum_fusion.1), channel_id=1, source_target_pairs={{0,1},{1,2},{2,3},{3,4},{4,5},{5,6},{6,7},{7,8},{8,9},{9,10},{10,1... | collective-permute-start | bytes 1253384 | tf_op jit(solution)/shard_map/ppermute | solution.py:18
  82.4 9.7 %collective-permute-start.8 = (f32[3,1,1,1024]{3,2,1,0:T(1,128)S(1)}, f32[3,1,1,1024]{3,2,1,0:T(1,128)S(1)}, u32[]{:S(2)}, u32[]{:S(2)}) collective-permute-start(f32[3,1,1,1024]{3,2,1,0:T(1,128)S(1)} %get-tuple-element.39), channel_id=1, source_target_pairs={{0,24},{24,48},{48,72},{72,96},{96,120},{120,144},{144,168},{168,1... | collective-permute-start | bytes 36872 | tf_op jit(solution)/shard_map/ppermute | solution.py:18
  86.4 6.5 %collective-permute-start.9 = (f32[3,1,1,1024]{3,2,1,0:T(1,128)S(1)}, f32[3,1,1,1024]{3,2,1,0:T(1,128)S(1)}, u32[]{:S(2)}, u32[]{:S(2)}) collective-permute-start(f32[3,1,1,1024]{3,2,1,0:T(1,128)S(1)} %get-tuple-element.40), channel_id=1, source_target_pairs={{24,0},{48,24},{72,48},{96,72},{120,96},{144,120},{168,144},{192,1... | collective-permute-start | bytes 36872 | tf_op jit(solution)/shard_map/ppermute | solution.py:20
  93.0 20.0 %collective-permute-start.11 = (f32[3,1,34,1024]{3,2,1,0:T(8,128)S(1)}, f32[3,1,34,1024]{3,2,1,0:T(8,128)S(1)}, u32[]{:S(2)}, u32[]{:S(2)}) collective-permute-start(f32[3,1,34,1024]{3,2,1,0:T(8,128)S(1)} %pad_maximum_fusion.2), channel_id=1, source_target_pairs={{1,0},{2,1},{3,2},{4,3},{5,4},{6,5},{7,6},{8,7},{9,8},{10,9},{11,1... | collective-permute-start | bytes 1253384 | tf_op jit(solution)/shard_map/ppermute | solution.py:20
  104.6 14.2 %collective-permute-start.10 = (f32[3,1,34,1024]{3,2,1,0:T(8,128)S(1)}, f32[3,1,34,1024]{3,2,1,0:T(8,128)S(1)}, u32[]{:S(2)}, u32[]{:S(2)}) collective-permute-start(f32[3,1,34,1024]{3,2,1,0:T(8,128)S(1)} %pad_maximum_fusion.2), channel_id=1, source_target_pairs={{0,1},{1,2},{2,3},{3,4},{4,5},{5,6},{6,7},{7,8},{8,9},{9,10},{10,1... | collective-permute-start | bytes 1253384 | tf_op jit(solution)/shard_map/ppermute | solution.py:18
  119.4 2.2 %copy-start.3 = (bf16[2,1024,1024]{2,1,0:T(8,128)(2,1)S(1)}, bf16[2,1024,1024]{2,1,0:T(8,128)(2,1)}, u32[]{:S(2)}) copy-start(bf16[2,1024,1024]{2,1,0:T(8,128)(2,1)} %param.6) | copy-start | bytes 12582916
  178.3 0.9 copy-start.2
where the time goes:
time: 181 us; the launch traced here: 180 us
  starting transfers between devices  72.9 us (40%)
  waiting for transfers between devices  38.2 us (21%)
  local copies, waits for them, and re-layouts  30 us (17%)
  blocking collectives  29.9 us (17%)
  other arithmetic  6.17 us (3%)
    ppermute x6, starting transfers between devices, extended(): lax.ppermute(head, axis, [((i + 1) % count, i) for i in range(count)])  56 us
    all_to_all x1, blocking collectives, body(): lax.all_to_all(x_pass, ('grp', 'row'), split_axis=2, concat_axis=3, tiled...  29.9 us
    ppermute x6, waiting for transfers between devices, extended(): lax.ppermute(head, axis, [((i + 1) % count, i) for i in range(count)])  20.6 us
    ppermute x6, waiting for transfers between devices, extended(): lax.ppermute(tail, axis, [(i, (i + 1) % count) for i in range(count)])  17.6 us
    ppermute x6, starting transfers between devices, extended(): lax.ppermute(tail, axis, [(i, (i + 1) % count) for i in range(count)])  16.9 us
    unnamed x10, local copies, waits for them, and re-layouts  14.2 us
    all_to_all x1, local copies, waits for them, and re-layouts, body(): lax.all_to_all(x_pass, ('grp', 'row'), split_axis=2, concat_axis=3, tiled...  5.3 us
    convert_element_type x1, local copies, waits for them, and re-layouts, body(): x_pass = jnp.einsum('yox,fyzx->fyoz', matrices, fields, preferred_element...  4.72 us
  transfers between devices with their start and end apart: 12, of which 9 were waited for; matrix products, arithmetic and copies ran while one was open for 0% of the time, Pallas kernels for 0%

commit v1 on v0

v1 whole, which is shorter than its diff:
```python
import functools

import jax
import jax.numpy as jnp
from jax import lax
from jax.experimental import pallas as pl
from jax.experimental.pallas import tpu as pltpu
from jax.sharding import PartitionSpec as P

F32 = jnp.float32
BF16 = jnp.bfloat16
MESH = pl.DeviceIdType.MESH
PRODUCT_PAIRS = ((0, 0), (0, 1), (0, 2), (1, 1), (1, 2), (2, 2))
FIELD_FACTORS = ((0,), (1,), (2,)) + PRODUCT_PAIRS

DEPTH = 3
HALF = 16
WIDE = HALF + 2 * DEPTH
ROWS = 2 + 2 * DEPTH
CELLS = ROWS * WIDE
DISTANCE = (3, 2, 1, 0, 0, 1, 2, 3)
CODE_MAX = 32767.0
BOUND = 8.0


def encode(value):
    root = jnp.sqrt(jnp.sqrt(jnp.abs(value) * (1.0 / BOUND)))
    code = (root * CODE_MAX + 0.5).astype(jnp.int32)
    return jnp.where(value < 0.0, -code, code).astype(jnp.int16)


def decode(code):
    root = code.astype(jnp.int32).astype(F32) * (1.0 / CODE_MAX)
    return (root * jnp.abs(root)) * (root * root * BOUND)


def kernel(
    sizes,
    profile_ref, velocity_ref, x_hbm, z_hbm, out_ref,
    spread, coded, gathered, wide, first, second, advanced, fields,
    x_mat, z_mat, send_main, send_last, recv_main, recv_last, z_pass,
    weight_sem, gather_send, gather_recv, local_sem, pass_send, pass_recv,
):
    n_grp, n_row, n_col = sizes
    n_blk, n_pln = n_grp * n_row, n_col // 2
    grp, row, col = lax.axis_index("grp"), lax.axis_index("row"), lax.axis_index("col")
    blk = grp * n_row + row
    pln, half = col // 2, col % 2
    other = 1 - half

    def device(block, plane, side):
        block = lax.rem(block + n_blk, n_blk)
        plane = lax.rem(plane + n_pln, n_pln)
        return (block // n_row, lax.rem(block, n_row), plane * 2 + side)

    barrier = pltpu.get_barrier_semaphore()

    def say(target):
        pl.semaphore_signal(barrier, inc=1, device_id=target, device_id_type=MESH)

    beside = blk - 1 + 2 * half
    for step in (-1, 1):
        for side in (0, 1):
            say(device(blk, pln + step, side))
            say(device(beside, pln + step, side))
    say(device(blk, pln - 2, 1))
    say(device(blk, pln + 2, 0))
    say(device(blk, pln, other))

    def say_block(step, carry):
        say(device(blk + step, pln, 0))
        say(device(blk + step, pln, 1))
        return carry

    lax.fori_loop(1, n_blk, say_block, 0)
    partners = 2 * n_blk - 1 + 10

    x_copy = pltpu.make_async_copy(x_hbm, x_mat, weight_sem.at[0])
    z_copy = pltpu.make_async_copy(z_hbm, z_mat, weight_sem.at[1])
    x_copy.start()
    z_copy.start()

    for comp in range(3):
        for group in range(4):
            for chunk in range(8):
                spread[comp, pl.ds(group * 64 + chunk, 8, stride=8), :] = velocity_ref[
                    comp, 0, group * 8:(group + 1) * 8, chunk * 128:(chunk + 1) * 128
                ]

    def encode_cell(cell, carry):
        start = pl.multiple_of(cell * 8, 8)
        for comp in range(3):
            coded[cell, comp] = encode(spread[comp, pl.ds(start, 8), :])
        return carry

    lax.fori_loop(0, 2 * HALF, encode_cell, 0)
    own_profile = jnp.full((8, 128), profile_ref[0], jnp.int32).astype(F32)
    for comp in range(3):
        coded[2 * HALF, comp] = own_profile.astype(jnp.int32).astype(jnp.int16)

    pl.semaphore_wait(barrier, partners)

    def give(source, count, place, target):
        pltpu.make_async_remote_copy(
            src_ref=coded.at[pl.ds(source, count)],
            dst_ref=gathered.at[pl.ds(place, count)],
            send_sem=gather_send, recv_sem=gather_recv,
            device_id=target, device_id_type=MESH,
        ).start()

    far_step = 4 * half - 2
    far_row = 7 * other
    for side in (0, 1):
        give(HALF * side, HALF, far_row * WIDE + DEPTH, device(blk, pln + far_step, side))
    for step in (-1, 1):
        place = (DEPTH + half - 2 * step) * WIDE
        give(0, HALF + 2, place + DEPTH, device(blk, pln + step, 0))
        give(HALF - 2, HALF + 2, place + DEPTH - 2, device(blk, pln + step, 1))
        give(2 * HALF - 2, 2, place + DEPTH - 2, device(blk + 1, pln + step, 0))
        give(0, 2, place + DEPTH + HALF, device(blk - 1, pln + step, 1))
    place = (DEPTH + half) * WIDE
    give(
        (HALF - DEPTH) * other, HALF + DEPTH, place + DEPTH - DEPTH * other,
        device(blk, pln, other),
    )
    give(2 * HALF - DEPTH, DEPTH, place, device(blk + 1, pln, 0))
    give(0, DEPTH, place + DEPTH + HALF, device(blk - 1, pln, 1))
    give(2 * HALF, 1, CELLS, device(blk, pln, other))
    own = pltpu.make_async_copy(
        coded.at[pl.ds((HALF - DEPTH) * half, HALF + DEPTH)],
        gathered.at[pl.ds(place + DEPTH - DEPTH * half, HALF + DEPTH)],
        local_sem.at[0],
    )
    own.start()
    own.wait()
    moved = 138
    pltpu.make_async_copy(
        gathered.at[pl.ds(0, moved)], gathered.at[pl.ds(0, moved)], gather_recv
    ).wait()

    inside = [
        jnp.where(
            (2 * pln - DEPTH + place_row >= 0) & (2 * pln - DEPTH + place_row < n_col), 1.0, 0.0
        ).astype(F32)
        for place_row in range(ROWS)
    ]

    for place_row in range(ROWS):
        reach = DEPTH - DISTANCE[place_row]

        def decode_cell(cell, carry, place_row=place_row):
            for comp in range(3):
                wide[place_row * WIDE + cell, comp] = (
                    decode(gathered[place_row * WIDE + cell, comp]) * inside[place_row]
                )
            return carry

        lax.fori_loop(DEPTH - reach, DEPTH + HALF + reach, decode_cell, 0)

    lane = lax.broadcasted_iota(jnp.int32, (8, 128), 1)
    last_lane, first_lane = lane == 127, lane == 0

    def stage(source, keep, old, store):
        weight, advect = 0.2 * keep, 0.125 * keep

        def cell_of(place_row, cell):
            here = place_row * WIDE + cell
            center = [source[here, comp] for comp in range(3)]
            pairs = []
            for comp in range(3):
                scaled = center[comp] * advect
                pairs.append((weight - scaled, weight + scaled))
            for comp in range(3):
                value = center[comp]
                ahead = pltpu.roll(value, 127, 1)
                ahead = jnp.where(last_lane, pltpu.roll(ahead, 7, 0), ahead)
                behind = pltpu.roll(value, 1, 1)
                behind = jnp.where(first_lane, pltpu.roll(behind, 1, 0), behind)
                total = (pairs[0][0] * ahead + pairs[0][1] * behind) + (
                    pairs[1][0] * source[here + WIDE, comp]
                    + pairs[1][1] * source[here - WIDE, comp]
                )
                total = total + (
                    pairs[2][0] * source[here + 1, comp] + pairs[2][1] * source[here - 1, comp]
                )
                total = total - weight * value
                if old:
                    total = total + old * wide[here, comp]
                store(place_row, cell, comp, total)

        return cell_of

    def sweep(number, cell_of):
        for place_row in range(ROWS):
            reach = DEPTH - number - DISTANCE[place_row]
            if reach < 0:
                continue

            def two(step, carry, place_row=place_row, low=DEPTH - reach):
                cell_of(place_row, low + 2 * step)
                cell_of(place_row, low + 2 * step + 1)
                return carry

            lax.fori_loop(0, (HALF + 2 * reach) // 2, two, 0)

    def into(target):
        def store(place_row, cell, comp, value):
            if DISTANCE[place_row]:
                value = value * inside[place_row]
            target[place_row * WIDE + cell, comp] = value

        return store

    def into_advanced(place_row, cell, comp, value):
        start = pl.multiple_of(((place_row - DEPTH) * HALF + cell - DEPTH) * 8, 8)
        advanced[comp, pl.ds(start, 8), :] = value

    sweep(1, stage(wide, 1.0, None, into(first)))
    sweep(2, stage(first, 0.25, 0.75, into(second)))
    sweep(3, stage(second, 2.0 / 3.0, 1.0 / 3.0, into_advanced))

    pair_profile = gathered[CELLS, 0].astype(jnp.int32).astype(F32)
    even = jnp.where(half == 0, own_profile, pair_profile)
    odd = jnp.where(half == 0, pair_profile, own_profile)
    one = jnp.concatenate([even, even, odd, odd], axis=0)
    zero = 1.0 - one
    for chunk in range(8):
        comps = [advanced[comp, pl.ds(chunk, 2 * HALF, stride=8), :] for comp in range(3)]
        for number, factors in enumerate(FIELD_FACTORS):
            field = functools.reduce(lambda a, b: a * b, [comps[f] for f in factors])
            rows = slice(number * 2 * HALF, (number + 1) * 2 * HALF)
            fields[rows, chunk * 128:(chunk + 1) * 128] = (field * zero).astype(BF16)
            fields[rows, 1024 + chunk * 128:1024 + (chunk + 1) * 128] = (field * one).astype(BF16)

    x_copy.wait()
    wide_lane = lax.broadcasted_iota(jnp.int32, (2 * HALF, 128), 1)
    quarter = wide_lane // 32
    small_quarter = lane // 32

    def outputs(step, carry):
        dest_grp = lax.rem(grp + 1 + step, n_grp)
        start = pl.multiple_of(dest_grp * n_row * 32, 256)
        contract = (((1,), (1,)), ((), ()))
        passed = lax.dot_general(
            fields[:, 0:1024], x_mat[0, pl.ds(start, 256), :], contract,
            preferred_element_type=F32,
        ) + lax.dot_general(
            fields[:, 1024:2048], x_mat[1, pl.ds(start, 256), :], contract,
            preferred_element_type=F32,
        )
        for tile in range(2):
            lanes = slice(tile * 128, (tile + 1) * 128)
            for part in range(2):
                turned = []
                for k in range(4):
                    piece = passed[(part * 4 + k) * 32:(part * 4 + k + 1) * 32, lanes]
                    turned.append(pltpu.roll(piece, 32 * k, 1) if k else piece)
                for place in range(4):
                    mixed = turned[3]
                    for k in range(3):
                        mixed = jnp.where(quarter == (place + k) % 4, turned[k], mixed)
                    mixed = mixed.astype(BF16)
                    dest = dest_grp * n_row + tile * 4 + place
                    send_main[part, dest] = mixed[0:HALF]
                    send_main[part, n_blk + dest] = mixed[HALF:2 * HALF]
            for line in range(2):
                low = passed[256 + line * HALF:256 + line * HALF + 8, lanes]
                high = pltpu.roll(passed[256 + line * HALF + 8:256 + (line + 1) * HALF, lanes], 32, 1)
                for place in range(4):
                    dest = dest_grp * n_row + tile * 4 + place
                    send_last[line * n_blk + dest] = jnp.where(
                        small_quarter == place, low, high
                    ).astype(BF16)
        spot = 2 * blk + half
        for off in (4, 3, 5, 2, 6, 1, 7, 0):
            dest_row = lax.rem(row + off, n_row)
            dest = dest_grp * n_row + dest_row
            for line in range(2):
                target = (dest_grp, dest_row, 2 * pln + line)

                def send(line=line, target=target, dest=dest):
                    for part in range(2):
                        pltpu.make_async_remote_copy(
                            src_ref=send_main.at[part, line * n_blk + dest],
                            dst_ref=recv_main.at[part, spot],
                            send_sem=pass_send.at[part], recv_sem=pass_recv.at[part],
                            device_id=target, device_id_type=MESH,
                        ).start()
                    pltpu.make_async_remote_copy(
                        src_ref=send_last.at[line * n_blk + dest],
                        dst_ref=recv_last.at[spot],
                        send_sem=pass_send.at[2], recv_sem=pass_recv.at[2],
                        device_id=target, device_id_type=MESH,
                    ).start()

                if off:
                    send()
                else:
                    pl.when((dest != blk) | (half != line))(send)
        return carry

    lax.fori_loop(0, n_grp, outputs, 0)
    spot = 2 * blk + half
    mine = half * n_blk + blk
    stays = [
        pltpu.make_async_copy(send_main.at[part, mine], recv_main.at[part, spot], local_sem.at[1 + part])
        for part in range(2)
    ]
    stays.append(pltpu.make_async_copy(send_last.at[mine], recv_last.at[spot], local_sem.at[3]))
    for stay in stays:
        stay.start()
    z_copy.wait()
    for stay in stays:
        stay.wait()

    contract = (((0,), (1,)), ((), ()))
    many = 2 * n_blk - 1
    for part in range(2):
        pltpu.make_async_copy(
            recv_main.at[part, pl.ds(0, many)], recv_main.at[part, pl.ds(0, many)], pass_recv.at[part]
        ).wait()
        lines = recv_main[part].reshape(2 * n_blk * HALF, 128)
        z_pass[part * 128:(part + 1) * 128, :] = lax.dot_general(
            lines, z_mat[...], contract, preferred_element_type=F32
        )
    pltpu.make_async_copy(
        recv_last.at[pl.ds(0, many)], recv_last.at[pl.ds(0, many)], pass_recv.at[2]
    ).wait()
    low = recv_last[...].astype(F32)
    high = pltpu.roll(low.reshape(2 * n_blk * 8, 128), 96, 1).reshape(2 * n_blk, 8, 128)
    lines = jnp.concatenate([low, high], axis=1).reshape(2 * n_blk * HALF, 128).astype(BF16)
    z_pass[256:384, :] = lax.dot_general(lines, z_mat[...], contract, preferred_element_type=F32)

    turn = lax.rem(row, 4)

    def filtered(number):
        part, k = number // 4, number % 4
        start = part * 128 + lax.rem(turn + k, 4) * 32
        return z_pass[pl.ds(pl.multiple_of(start, 32), 32), :]

    linear = [filtered(number) for number in range(3)]
    for number, (left, right) in enumerate(PRODUCT_PAIRS):
        out_ref[number, 0] = filtered(3 + number) - linear[left] * linear[right]

    pltpu.make_async_copy(
        gathered.at[pl.ds(0, moved)], gathered.at[pl.ds(0, moved)], gather_send
    ).wait()
    for part in range(2):
        pltpu.make_async_copy(
            send_main.at[part, pl.ds(0, many)], send_main.at[part, pl.ds(0, many)], pass_send.at[part]
        ).wait()
    pltpu.make_async_copy(
        send_last.at[pl.ds(0, many)], send_last.at[pl.ds(0, many)], pass_send.at[2]
    ).wait()


def solution(mesh):
    sizes = (mesh.shape["grp"], mesh.shape["row"], mesh.shape["col"])
    n_blk = sizes[0] * sizes[1]
    tile = (8, 128)

    def body(velocity, profile, x_filters, z_filter):
        vmem = pl.BlockSpec(memory_space=pltpu.VMEM)
        return pl.pallas_call(
            functools.partial(kernel, sizes),
            out_shape=jax.ShapeDtypeStruct((6, 1, 32, 1024), F32),
            in_specs=[
                pl.BlockSpec(memory_space=pltpu.SMEM),
                vmem,
                pl.BlockSpec(memory_space=pl.ANY),
                pl.BlockSpec(memory_space=pl.ANY),
            ],
            out_specs=vmem,
            scratch_shapes=[
                pltpu.VMEM((3, 256, 128), F32),
                pltpu.VMEM((2 * HALF + 1, 3) + tile, jnp.int16),
                pltpu.VMEM((CELLS + 1, 3) + tile, jnp.int16),
                pltpu.VMEM((CELLS, 3) + tile, F32),
                pltpu.VMEM((CELLS, 3) + tile, F32),
                pltpu.VMEM((CELLS, 3) + tile, F32),
                pltpu.VMEM((3, 256, 128), F32),
                pltpu.VMEM((9 * 2 * HALF, 2048), BF16),
                pltpu.VMEM((2, 1024, 1024), BF16),
                pltpu.VMEM((1024, 1024), BF16),
                pltpu.VMEM((2, 2 * n_blk, HALF, 128), BF16),
                pltpu.VMEM((2 * n_blk, 8, 128), BF16),
                pltpu.VMEM((2, 2 * n_blk, HALF, 128), BF16),
                pltpu.VMEM((2 * n_blk, 8, 128), BF16),
                pltpu.VMEM((384, 1024), F32),
                pltpu.SemaphoreType.DMA((2,)),
                pltpu.SemaphoreType.DMA,
                pltpu.SemaphoreType.DMA,
                pltpu.SemaphoreType.DMA((4,)),
                pltpu.SemaphoreType.DMA((3,)),
                pltpu.SemaphoreType.DMA((3,)),
            ],
            compiler_params=pltpu.CompilerParams(
                collective_id=0, has_side_effects=True, vmem_limit_bytes=60000 * 1024
            ),
            name="subgrid",
        )(profile, velocity, x_filters, z_filter)

    placed = (P(None, "col", ("grp", "row"), None), P("col"), P(), P())
    return jax.shard_map(
        body,
        mesh=mesh,
        in_specs=placed,
        out_specs=P(None, "col", ("grp", "row"), None),
        check_vma=False,
    )
```

time: 181 us -> 73.6 us (0.41)
  starting transfers between devices: 72.9 us -> 0 us
  Pallas kernels: 0 us -> 70.7 us
  waiting for transfers between devices: 38.2 us -> 0 us
  blocking collectives: 29.9 us -> 0 us
  local copies, waits for them, and re-layouts: 30 us -> 2.09 us
  other arithmetic: 6.17 us -> 0 us
    ppermute x12 -> x0, starting transfers between devices: 72.9 us -> none  [the longest x6 56 us: extended(): lax.ppermute(head, axis, [((i + 1) % count, i) for i in range(count)])]
    pallas_call x0 -> x1, Pallas kernels: none -> 70.7 us  [body(): pl.pallas_call(functools.partial(kernel, sizes), out_shape=jax.ShapeDtype...]
    ppermute x12 -> x0, waiting for transfers between devices: 38.2 us -> none  [the longest x6 20.6 us: extended(): lax.ppermute(head, axis, [((i + 1) % count, i) for i in range(count)])]
    all_to_all x1 -> x0, blocking collectives: 29.9 us -> none  [body(): lax.all_to_all(x_pass, ('grp', 'row'), split_axis=2, concat_axis=3, tiled...]
    unnamed x10 -> x1, local copies, waits for them, and re-layouts: 14.2 us -> 2.09 us
    all_to_all x1 -> x0, local copies, waits for them, and re-layouts: 5.3 us -> none  [body(): lax.all_to_all(x_pass, ('grp', 'row'), split_axis=2, concat_axis=3, tiled...]
    convert_element_type x1 -> x0, local copies, waits for them, and re-layouts: 4.72 us -> none  [body(): x_pass = jnp.einsum('yox,fyzx->fyoz', matrices, fields, preferred_element...]
    another operation x1 -> x0, local copies, waits for them, and re-layouts: 3.88 us -> none
  transfers between devices with their start and end apart: 12 -> 0, of which waited for: 9 -> 0; matrix products, arithmetic and copies ran while one was open for 0% -> 0% of each run, Pallas kernels for 0% -> 0%
where the time goes in v1:
time: 73.6 us; the launch traced here: 73.4 us
  Pallas kernels  70.7 us (96%)
  local copies, waits for them, and re-layouts  2.09 us (3%)
    pallas_call x1, Pallas kernels, body(): pl.pallas_call(functools.partial(kernel, sizes), out_shape=jax.ShapeDtype...  70.7 us
    unnamed x1, local copies, waits for them, and re-layouts  2.09 us

profile of v1, /device:TPU:1, one launch (start us, length us, event | category | flops | bytes accessed | tf_op | source)
XLA Modules:
  0.0 73.4 jit_solution(15742015074698037573)
XLA Ops:
  0.7 70.7 %subgrid.1 = f32[6,1,32,1024]{3,2,1,0:T(8,128)} custom-call(s32[1]{0:T(128)S(6)} %copy.6.profile_ref, f32[3,1,32,1024]{3,2,1,0:T(8,128)} %velocity_ref.1, bf16[2,1024,1024]{2,1,0:T(8,128)(2,1)} %x_hbm.1, bf16[1024,1024]{1,0:T(8,128)(2,1)} %z_hbm.1), custom_call_target="tpu_custom_call" | custom-call | tf_op jit(solution)/shard_map/subgrid/pallas_call | solution.py:364
  71.3 2.1 %copy.7 = f32[6,1,32,1024]{3,2,1,0:T(8,128)} copy(f32[6,1,32,1024]{3,2,1,0:T(8,128)} %subgrid.1) | data formatting | bytes 1572864

commit v2 on v0

v2 whole, which is shorter than its diff:
```python
import functools

import jax
import jax.numpy as jnp
from jax import lax
from jax.experimental import pallas as pl
from jax.experimental.pallas import tpu as pltpu
from jax.sharding import PartitionSpec as P

F32 = jnp.float32
BF16 = jnp.bfloat16
MESH = pl.DeviceIdType.MESH
PRODUCT_PAIRS = ((0, 0), (0, 1), (0, 2), (1, 1), (1, 2), (2, 2))
FIELD_FACTORS = ((0,), (1,), (2,)) + PRODUCT_PAIRS

DEPTH = 3
HALF = 16
PART = 8
WIDE = HALF + 2 * DEPTH
ROWS = 2 + 2 * DEPTH
CELLS = ROWS * WIDE
CODE_MAX = 32767.0
BOUND = 8.0


def encode(value):
    root = jnp.sqrt(jnp.sqrt(jnp.abs(value) * (1.0 / BOUND)))
    code = (root * CODE_MAX + 0.5).astype(jnp.int32)
    return jnp.where(value < 0.0, -code, code).astype(jnp.int16)


def decode(code):
    root = code.astype(jnp.int32).astype(F32) * (1.0 / CODE_MAX)
    return (root * jnp.abs(root)) * (root * root * BOUND)


def kernel(
    sizes,
    profile_ref, velocity_ref, x_hbm, z_hbm, direct_ref, product_ref,
    spread, coded, gathered, wide, first, second, advanced, fields, last_low,
    x_mat, z_mat, send_first, send_second, recv_first, recv_second, z_pass,
    weight_sem, gather_send, gather_recv, profile_sem, local_sem, pass_send, pass_recv,
):
    n_grp, n_row, n_col = sizes
    n_blk, n_pln = n_grp * n_row, n_col // 2
    grp, row, col = lax.axis_index("grp"), lax.axis_index("row"), lax.axis_index("col")
    blk = grp * n_row + row
    pln, half = col // 2, col % 2
    other = 1 - half
    toward = 2 * half - 1

    def there(plane):
        return (plane >= 0) & (plane < n_pln)

    def device(block, plane, side):
        block = lax.rem(block + n_blk, n_blk)
        return (block // n_row, lax.rem(block, n_row), plane * 2 + side)

    barrier = pltpu.get_barrier_semaphore()

    def say(target):
        pl.semaphore_signal(barrier, inc=1, device_id=target, device_id_type=MESH)

    beside = blk + toward
    for step in (-1, 1):
        @pl.when(there(pln + step))
        def _(step=step):
            for side in (0, 1):
                say(device(blk, pln + step, side))
                say(device(beside, pln + step, side))

    @pl.when(there(pln - 2))
    def _():
        say(device(blk, pln - 2, 1))

    @pl.when(there(pln + 2))
    def _():
        say(device(blk, pln + 2, 0))

    say(device(blk, pln, other))

    def say_block(step, carry):
        say(device(blk + step, pln, 0))
        say(device(blk + step, pln, 1))
        return carry

    lax.fori_loop(1, n_blk, say_block, 0)

    x_copy = pltpu.make_async_copy(x_hbm, x_mat, weight_sem.at[0])
    z_copy = pltpu.make_async_copy(z_hbm, z_mat, weight_sem.at[1])
    x_copy.start()
    z_copy.start()

    for group in range(4):
        for comp in range(3):
            for chunk in range(8):
                spread[comp, pl.ds(group * 64 + chunk, 8, stride=8), :] = velocity_ref[
                    comp, 0, group * 8:(group + 1) * 8, chunk * 128:(chunk + 1) * 128
                ]

    def encode_cells(step, carry):
        for cell in range(4):
            start = pl.multiple_of((step * 4 + cell) * 8, 8)
            for comp in range(3):
                coded[step * 4 + cell, comp] = encode(spread[comp, pl.ds(start, 8), :])
        return carry

    lax.fori_loop(0, 2 * HALF // 4, encode_cells, 0)
    own_profile = jnp.full((8, 128), profile_ref[0], jnp.int32)
    for comp in range(3):
        coded[2 * HALF, comp] = own_profile.astype(jnp.int16)

    partners = 2 * n_blk - 1
    for step, count in ((toward, 4), (-toward, 4), (2 * toward, 2)):
        partners = partners + jnp.where(there(pln + step), count, 0)
    pl.semaphore_wait(barrier, partners)

    def give(source, count, cell, part, line, kind, target):
        pltpu.make_async_remote_copy(
            src_ref=coded.at[pl.ds(source, count)],
            dst_ref=gathered.at[pl.ds(line * WIDE + cell, count)],
            send_sem=gather_send.at[kind], recv_sem=gather_recv.at[part, line],
            device_id=target, device_id_type=MESH,
        ).start()

    pltpu.make_async_remote_copy(
        src_ref=coded.at[pl.ds(2 * HALF, 1)], dst_ref=gathered.at[pl.ds(CELLS, 1)],
        send_sem=gather_send.at[4], recv_sem=profile_sem,
        device_id=device(blk, pln, other), device_id_type=MESH,
    ).start()

    own_line = DEPTH + half
    lines = (own_line, 5 - 3 * half, 1 + 5 * half, 7 - 7 * half)
    steps = (0, toward, -toward, 2 * toward)
    for part in range(2):
        for d in range(4):
            def main(side, d=d, part=part):
                target = device(blk, pln + steps[d], side)
                if part == 0 and side == 0:
                    give(0, 11 - d, DEPTH, part, lines[d], d, target)
                elif part == 0:
                    give(13 + d, 14 - 2 * d, d, part, lines[d], d, target)
                elif side == 0:
                    give(11 - d, PART, 14 - d, part, lines[d], d, target)
                else:
                    give(27 - d, 5 + d, 14 - d, part, lines[d], d, target)

            def strip(d=d, part=part):
                if d == 3:
                    return
                if part == 0:
                    give(29 + d, 3 - d, d, part, lines[d], d, device(blk + 1, pln + steps[d], 0))
                else:
                    give(0, 3 - d, DEPTH + HALF, part, lines[d], d, device(blk - 1, pln + steps[d], 1))

            if d == 0:
                for side in (0, 1):
                    pl.when(half != side)(functools.partial(main, side))
                strip()
            else:
                @pl.when(there(pln + steps[d]))
                def _(main=main, strip=strip):
                    main(0)
                    main(1)
                    strip()

    present = [
        (2 * pln - DEPTH + line >= 0) & (2 * pln - DEPTH + line < n_col) for line in range(ROWS)
    ]
    inside = [jnp.where(known, 1.0, 0.0).astype(F32) for known in present]

    for line in (0, 1, 2, 5, 6, 7):
        @pl.when(jnp.logical_not(present[line]))
        def _(line=line):
            def clear(cell, carry):
                for comp in range(3):
                    wide[line * WIDE + cell, comp] = jnp.zeros((8, 128), F32)
                return carry

            lax.fori_loop(0, WIDE, clear, 0)

    def keep(cell, carry):
        start = pl.multiple_of(((HALF - DEPTH) * half + cell) * 8, 8)
        for comp in range(3):
            wide[own_line * WIDE + DEPTH * other + cell, comp] = spread[comp, pl.ds(start, 8), :]
        return carry

    lax.fori_loop(0, HALF + DEPTH, keep, 0)

    def arrive(part, line, low, count):
        pltpu.make_async_copy(
            gathered.at[pl.ds(0, count)], gathered.at[pl.ds(0, count)], gather_recv.at[part, line]
        ).wait()
        per = 2 if count % 2 == 0 else 1

        def some(step, carry):
            for cell in range(per):
                here = line * WIDE + low + step * per + cell
                for comp in range(3):
                    wide[here, comp] = decode(gathered[here, comp])
            return carry

        lax.fori_loop(0, count // per, some, 0)

    lane = lax.broadcasted_iota(jnp.int32, (8, 128), 1)
    last_lane, first_lane = lane == 127, lane == 0

    def advance(source, scale, old, here):
        weight, advect = 0.2 * scale, 0.125 * scale
        center = [source[here, comp] for comp in range(3)]
        pairs = []
        for comp in range(3):
            scaled = center[comp] * advect
            pairs.append((weight - scaled, weight + scaled))
        results = []
        for comp in range(3):
            value = center[comp]
            ahead = pltpu.roll(value, 127, 1)
            ahead = jnp.where(last_lane, pltpu.roll(ahead, 7, 0), ahead)
            behind = pltpu.roll(value, 1, 1)
            behind = jnp.where(first_lane, pltpu.roll(behind, 1, 0), behind)
            total = (pairs[0][0] * ahead + pairs[0][1] * behind) + (
                pairs[1][0] * source[here + WIDE, comp] + pairs[1][1] * source[here - WIDE, comp]
            )
            total = total + (
                pairs[2][0] * source[here + 1, comp] + pairs[2][1] * source[here - 1, comp]
            )
            total = total - weight * value
            if old:
                total = total + old * wide[here, comp]
            results.append(total)
        return results

    def sweep(number, part, d):
        source = (wide, first, second)[number - 1]
        scale, old = ((1.0, None), (0.25, 0.75), (2.0 / 3.0, 1.0 / 3.0))[number - 1]
        low, high = ((d + number, 14 - d - number), (14 - d - number, 22 - d - number))[part]

        def two(step, carry):
            done = []
            for line in (DEPTH - d, DEPTH + 1 + d):
                for cell in range(2):
                    place = low + 2 * step + cell
                    done.append((line, place, advance(source, scale, old, line * WIDE + place)))
            for line, place, results in done:
                for comp in range(3):
                    value = results[comp]
                    if number == 3:
                        start = ((part * 2 + line - DEPTH) * PART + place - low) * 8
                        advanced[comp, pl.ds(pl.multiple_of(start, 8), 8), :] = value
                        continue
                    if d:
                        value = value * inside[line]
                    (first, second)[number - 1][line * WIDE + place, comp] = value
            return carry

        lax.fori_loop(0, (high - low) // 2, two, 0)

    wide_lane = lax.broadcasted_iota(jnp.int32, (2 * PART, 128), 1)
    quarter = wide_lane // 32
    small_quarter = lane // 32
    spot = 2 * blk + half

    def pass_part(part, one, zero):
        for chunk in range(8):
            comps = [
                advanced[comp, pl.ds(part * 128 + chunk, 2 * PART, stride=8), :] for comp in range(3)
            ]
            for number, factors in enumerate(FIELD_FACTORS):
                field = functools.reduce(lambda a, b: a * b, [comps[f] for f in factors])
                rows = slice(number * 2 * PART, (number + 1) * 2 * PART)
                fields[rows, chunk * 128:(chunk + 1) * 128] = (field * zero).astype(BF16)
                fields[rows, 1024 + chunk * 128:1024 + (chunk + 1) * 128] = (field * one).astype(BF16)
        send_ref = (send_first, send_second)[part]
        recv_ref = (recv_first, recv_second)[part]

        def outputs(step, carry):
            dest_grp = lax.rem(grp + 1 + step, n_grp)
            start = pl.multiple_of(dest_grp * n_row * 32, 256)
            contract = (((1,), (1,)), ((), ()))
            passed = lax.dot_general(
                fields[:, 0:1024], x_mat[0, pl.ds(start, 256), :], contract,
                preferred_element_type=F32,
            ) + lax.dot_general(
                fields[:, 1024:2048], x_mat[1, pl.ds(start, 256), :], contract,
                preferred_element_type=F32,
            )
            if part == 0:
                last_low[:, pl.ds(start, 256)] = passed[128:144]
            else:
                lows = last_low[:, pl.ds(start, 256)]
            for tile in range(2):
                lanes = slice(tile * 128, (tile + 1) * 128)
                for four in range(2):
                    turned = []
                    for k in range(4):
                        piece = passed[(four * 4 + k) * 16:(four * 4 + k + 1) * 16, lanes]
                        turned.append(pltpu.roll(piece, 32 * k, 1) if k else piece)
                    for place in range(4):
                        mixed = turned[3]
                        for k in range(3):
                            mixed = jnp.where(quarter == (place + k) % 4, turned[k], mixed)
                        dest = dest_grp * n_row + tile * 4 + place
                        send_ref[dest, four] = mixed[0:PART].astype(BF16)
                        send_ref[n_blk + dest, four] = mixed[PART:2 * PART].astype(BF16)
                if part == 1:
                    for line in range(2):
                        rows = slice(line * PART, (line + 1) * PART)
                        high = pltpu.roll(passed[128:144, lanes][rows], 32, 1)
                        low = lows[rows, lanes]
                        for place in range(4):
                            dest = dest_grp * n_row + tile * 4 + place
                            send_ref[line * n_blk + dest, 2] = jnp.where(
                                small_quarter == place, low, high
                            ).astype(BF16)
            for off in (4, 3, 5, 2, 6, 1, 7, 0):
                dest_row = lax.rem(row + off, n_row)
                dest = dest_grp * n_row + dest_row
                for line in range(2):
                    target = (dest_grp, dest_row, 2 * pln + line)

                    def send(line=line, target=target, dest=dest):
                        pltpu.make_async_remote_copy(
                            src_ref=send_ref.at[line * n_blk + dest], dst_ref=recv_ref.at[spot],
                            send_sem=pass_send.at[part], recv_sem=pass_recv.at[part],
                            device_id=target, device_id_type=MESH,
                        ).start()

                    if off:
                        send()
                    else:
                        pl.when((dest != blk) | (half != line))(send)
            return carry

        lax.fori_loop(0, n_grp, outputs, 0)
        stay = pltpu.make_async_copy(
            send_ref.at[half * n_blk + blk], recv_ref.at[spot], local_sem.at[part]
        )
        stay.start()
        return stay

    stays = []
    for part in range(2):
        for d in range(4):
            if d == 0:
                arrive(part, 4 - half, (0, 14)[part], (14, PART)[part])
                pl.when(half == part)(
                    functools.partial(arrive, part, own_line, (0, DEPTH + HALF)[part], DEPTH)
                )
                continue
            for line in (DEPTH - d, DEPTH + 1 + d):
                pl.when(present[line])(
                    functools.partial(arrive, part, line, (d, 14 - d)[part], (14 - 2 * d, PART)[part])
                )
            for number in range(1, d + 1):
                sweep(number, part, d - number)
        if part == 0:
            pltpu.make_async_copy(
                gathered.at[pl.ds(0, 1)], gathered.at[pl.ds(0, 1)], profile_sem
            ).wait()
            pair_profile = gathered[CELLS, 0].astype(jnp.int32)
            even = jnp.where(half == 0, own_profile, pair_profile).astype(F32)
            odd = jnp.where(half == 0, pair_profile, own_profile).astype(F32)
            one = jnp.concatenate([even, odd], axis=0)
            x_copy.wait()
        stays.append(pass_part(part, one, 1.0 - one))
    z_copy.wait()

    contract = (((0,), (1,)), ((), ()))
    many = 2 * n_blk - 1
    for part, ref in ((0, recv_first), (1, recv_second)):
        stays[part].wait()
        pltpu.make_async_copy(
            ref.at[pl.ds(0, many)], ref.at[pl.ds(0, many)], pass_recv.at[part]
        ).wait()

    def z_filter(number, low, high):
        cells = jnp.concatenate([low, high], axis=1).reshape(2 * n_blk * HALF, 128).astype(BF16)
        z_pass[number * 128:(number + 1) * 128, :] = lax.dot_general(
            cells, z_mat[...], contract, preferred_element_type=F32
        )

    for four in range(2):
        z_filter(four, recv_first[:, four].astype(F32), recv_second[:, four].astype(F32))
    low = recv_second[:, 2].astype(F32)
    high = pltpu.roll(low.reshape(2 * n_blk * PART, 128), 96, 1).reshape(2 * n_blk, PART, 128)
    z_filter(2, low, high)

    turn = lax.rem(row, 4)

    def filtered(number):
        start = (number // 4) * 128 + lax.rem(turn + number % 4, 4) * 32
        return z_pass[pl.ds(pl.multiple_of(start, 32), 32), :]

    linear = [filtered(number) for number in range(3)]
    for number, (left, right) in enumerate(PRODUCT_PAIRS):
        direct_ref[number, 0] = filtered(3 + number)
        product_ref[number, 0] = linear[left] * linear[right]

    def sent(sem, count):
        pltpu.make_async_copy(gathered.at[pl.ds(0, count)], gathered.at[pl.ds(0, count)], sem).wait()

    sent(gather_send.at[4], 1)
    sent(gather_send.at[0], 25)
    for d, count in ((1, 40), (2, 36), (3, 32)):
        pl.when(there(pln + steps[d]))(functools.partial(sent, gather_send.at[d], count))
    for part, ref in ((0, send_first), (1, send_second)):
        pltpu.make_async_copy(
            ref.at[pl.ds(0, many)], ref.at[pl.ds(0, many)], pass_send.at[part]
        ).wait()


def solution(mesh):
    sizes = (mesh.shape["grp"], mesh.shape["row"], mesh.shape["col"])
    n_blk = sizes[0] * sizes[1]
    tile = (8, 128)

    def body(velocity, profile, x_filters, z_filter):
        vmem = pl.BlockSpec(memory_space=pltpu.VMEM)
        result = jax.ShapeDtypeStruct((6, 1, 32, 1024), F32)
        direct, product = pl.pallas_call(
            functools.partial(kernel, sizes),
            out_shape=(result, result),
            in_specs=[
                pl.BlockSpec(memory_space=pltpu.SMEM),
                vmem,
                pl.BlockSpec(memory_space=pl.ANY),
                pl.BlockSpec(memory_space=pl.ANY),
            ],
            out_specs=(vmem, vmem),
            scratch_shapes=[
                pltpu.VMEM((3, 256, 128), F32),
                pltpu.VMEM((2 * HALF + 1, 3) + tile, jnp.int16),
                pltpu.VMEM((CELLS + 1, 3) + tile, jnp.int16),
                pltpu.VMEM((CELLS, 3) + tile, F32),
                pltpu.VMEM((CELLS, 3) + tile, F32),
                pltpu.VMEM((CELLS, 3) + tile, F32),
                pltpu.VMEM((3, 256, 128), F32),
                pltpu.VMEM((9 * 2 * PART, 2048), BF16),
                pltpu.VMEM((2 * PART, 1024), F32),
                pltpu.VMEM((2, 1024, 1024), BF16),
                pltpu.VMEM((1024, 1024), BF16),
                pltpu.VMEM((2 * n_blk, 2) + tile, BF16),
                pltpu.VMEM((2 * n_blk, 3) + tile, BF16),
                pltpu.VMEM((2 * n_blk, 2) + tile, BF16),
                pltpu.VMEM((2 * n_blk, 3) + tile, BF16),
                pltpu.VMEM((384, 1024), F32),
                pltpu.SemaphoreType.DMA((2,)),
                pltpu.SemaphoreType.DMA((5,)),
                pltpu.SemaphoreType.DMA((2, ROWS)),
                pltpu.SemaphoreType.DMA,
                pltpu.SemaphoreType.DMA((2,)),
                pltpu.SemaphoreType.DMA((2,)),
                pltpu.SemaphoreType.DMA((2,)),
            ],
            compiler_params=pltpu.CompilerParams(
                collective_id=0, has_side_effects=True, vmem_limit_bytes=60000 * 1024
            ),
            name="subgrid",
        )(profile, velocity, x_filters, z_filter)
        return direct - product

    placed = (P(None, "col", ("grp", "row"), None), P("col"), P(), P())
    return jax.shard_map(
        body,
        mesh=mesh,
        in_specs=placed,
        out_specs=P(None, "col", ("grp", "row"), None),
        check_vma=False,
    )
```

time: 181 us -> 48.5 us (0.27)
  starting transfers between devices: 72.9 us -> 0 us
  Pallas kernels: 0 us -> 45 us
  waiting for transfers between devices: 38.2 us -> 0 us
  local copies, waits for them, and re-layouts: 30 us -> 0 us
  blocking collectives: 29.9 us -> 0 us
  other arithmetic: 6.17 us -> 2.37 us
    ppermute x12 -> x0, starting transfers between devices: 72.9 us -> none  [the longest x6 56 us: extended(): lax.ppermute(head, axis, [((i + 1) % count, i) for i in range(count)])]
    pallas_call x0 -> x1, Pallas kernels: none -> 45 us  [body(): pl.pallas_call(functools.partial(kernel, sizes), out_shape=(result, resul...]
    ppermute x12 -> x0, waiting for transfers between devices: 38.2 us -> none  [the longest x6 20.6 us: extended(): lax.ppermute(head, axis, [((i + 1) % count, i) for i in range(count)])]
    all_to_all x1 -> x0, blocking collectives: 29.9 us -> none  [body(): lax.all_to_all(x_pass, ('grp', 'row'), split_axis=2, concat_axis=3, tiled...]
    unnamed x10 -> x0, local copies, waits for them, and re-layouts: 14.2 us -> none
    all_to_all x1 -> x0, local copies, waits for them, and re-layouts: 5.3 us -> none  [body(): lax.all_to_all(x_pass, ('grp', 'row'), split_axis=2, concat_axis=3, tiled...]
    convert_element_type x1 -> x0, local copies, waits for them, and re-layouts: 4.72 us -> none  [body(): x_pass = jnp.einsum('yox,fyzx->fyoz', matrices, fields, preferred_element...]
    another operation x1 -> x0, local copies, waits for them, and re-layouts: 3.88 us -> none
  transfers between devices with their start and end apart: 12 -> 0, of which waited for: 9 -> 0; matrix products, arithmetic and copies ran while one was open for 0% -> 0% of each run, Pallas kernels for 0% -> 0%
where the time goes in v2:
time: 48.5 us; the launch traced here: 48 us
  Pallas kernels  45 us (93%)
  other arithmetic  2.37 us (5%)
  between operations  0.66 us (1%)
    pallas_call x1, Pallas kernels, body(): pl.pallas_call(functools.partial(kernel, sizes), out_shape=(result, resul...  45 us
    sub x1, other arithmetic, body(): return direct - product  2.37 us

profile of v2, /device:TPU:1, one launch (start us, length us, event | category | flops | bytes accessed | tf_op | source)
XLA Modules:
  0.0 48.0 jit_solution(5216250997231156585)
XLA Ops:
  0.7 45.0 %subgrid.1 = (f32[6,1,32,1024]{3,2,1,0:T(8,128)}, f32[6,1,32,1024]{3,2,1,0:T(8,128)}) custom-call(s32[1]{0:T(128)S(6)} %copy.5.profile_ref, f32[3,1,32,1024]{3,2,1,0:T(8,128)} %velocity_ref.1, bf16[2,1024,1024]{2,1,0:T(8,128)(2,1)} %x_hbm.1, bf16[1024,1024]{1,0:T(8,128)(2,1)} %z_hbm.1), custom_call_target="tpu_custom_call" | custom-call | tf_op jit(solution)/shard_map/subgrid/pallas_call | solution.py:421
  45.6 2.4 %sub.3 = f32[6,1,32,1024]{3,2,1,0:T(8,128)} subtract(f32[6,1,32,1024]{3,2,1,0:T(8,128)} %get-tuple-element.7, f32[6,1,32,1024]{3,2,1,0:T(8,128)} %get-tuple-element.8) | non-fusion elementwise | flops 196608 | bytes 2359296 | tf_op jit(solution)/shard_map/sub | solution.py:461

commit v3 on v2

--- a/solution.py
+++ b/solution.py
@@ -39,7 +39,7 @@
     profile_ref, velocity_ref, x_hbm, z_hbm, direct_ref, product_ref,
     spread, coded, gathered, wide, first, second, advanced, fields, last_low,
     x_mat, z_mat, send_first, send_second, recv_first, recv_second, z_pass,
-    weight_sem, gather_send, gather_recv, profile_sem, local_sem, pass_send, pass_recv,
+    weight_sem, gather_send, gather_recv, profile_sem, local_sem, pass_send, pass_recv, word,
 ):
     n_grp, n_row, n_col = sizes
     n_blk, n_pln = n_grp * n_row, n_col // 2
@@ -77,14 +77,16 @@
     def _():
         say(device(blk, pln + 2, 0))
 
-    say(device(blk, pln, other))
-
-    def say_block(step, carry):
-        say(device(blk + step, pln, 0))
-        say(device(blk + step, pln, 1))
-        return carry
-
-    lax.fori_loop(1, n_blk, say_block, 0)
+    around = [(grp, lax.rem(row + step, n_row), col) for step in (1, n_row - 1)]
+    across = [
+        (grp, row, pln * 2 + other),
+        (grp + 1 - 2 * lax.rem(grp, 2), row, col),
+        (lax.rem(grp + 2, n_grp), row, col),
+    ]
+    for target in around + across:
+        say(target)
+    for side in (0, 1):
+        say(device(beside, pln, side))
 
     x_copy = pltpu.make_async_copy(x_hbm, x_mat, weight_sem.at[0])
     z_copy = pltpu.make_async_copy(z_hbm, z_mat, weight_sem.at[1])
@@ -110,7 +112,7 @@
     for comp in range(3):
         coded[2 * HALF, comp] = own_profile.astype(jnp.int16)
 
-    partners = 2 * n_blk - 1
+    partners = 7
     for step, count in ((toward, 4), (-toward, 4), (2 * toward, 2)):
         partners = partners + jnp.where(there(pln + step), count, 0)
     pl.semaphore_wait(barrier, partners)
@@ -186,6 +188,17 @@
         return carry
 
     lax.fori_loop(0, HALF + DEPTH, keep, 0)
+
+    def tell(target, turn):
+        pl.semaphore_signal(word.at[turn], inc=1, device_id=target, device_id_type=MESH)
+
+    for turn in range(n_row // 2):
+        for target in around:
+            tell(target, turn)
+        pl.semaphore_wait(word.at[turn], 2)
+    for turn, target in enumerate(across):
+        tell(target, n_row // 2 + turn)
+        pl.semaphore_wait(word.at[n_row // 2 + turn], 1)
 
     def arrive(part, line, low, count):
         pltpu.make_async_copy(
@@ -417,7 +430,7 @@
 
     def body(velocity, profile, x_filters, z_filter):
         vmem = pl.BlockSpec(memory_space=pltpu.VMEM)
-        result = jax.ShapeDtypeStruct((6, 1, 32, 1024), F32)
+        result = pltpu.VMEM((6, 1, 32, 1024), F32)
         direct, product = pl.pallas_call(
             functools.partial(kernel, sizes),
             out_shape=(result, result),
@@ -452,6 +465,7 @@
                 pltpu.SemaphoreType.DMA((2,)),
                 pltpu.SemaphoreType.DMA((2,)),
                 pltpu.SemaphoreType.DMA((2,)),
+                pltpu.SemaphoreType.REGULAR((sizes[1] // 2 + 3,)),
             ],
             compiler_params=pltpu.CompilerParams(
                 collective_id=0, has_side_effects=True, vmem_limit_bytes=60000 * 1024

time: 48.5 us -> 47.4 us (0.977)
  other arithmetic: 2.37 us -> 1 us
  Pallas kernels: 45 us -> 45.6 us
    sub x1, other arithmetic: 2.37 us -> 1 us  [body(): return direct - product]
    pallas_call x1, Pallas kernels: 45 us -> 45.6 us  [body(): pl.pallas_call(functools.partial(kernel, sizes), out_shape=(result, resul...]
where the time goes in v3:
time: 47.4 us; the launch traced here: 47.3 us
  Pallas kernels  45.6 us (96%)
  other arithmetic  1 us (2%)
  between operations  0.66 us (1%)
    pallas_call x1, Pallas kernels, body(): pl.pallas_call(functools.partial(kernel, sizes), out_shape=(result, resul...  45.6 us
    sub x1, other arithmetic, body(): return direct - product  1 us

profile of v3, /device:TPU:1, one launch (start us, length us, event | category | flops | bytes accessed | tf_op | source)
XLA Modules:
  0.0 47.3 jit_solution(13565614108922599272)
XLA Ops:
  0.7 45.6 %subgrid.1 = (f32[6,1,32,1024]{3,2,1,0:T(8,128)S(1)}, f32[6,1,32,1024]{3,2,1,0:T(8,128)S(1)}) custom-call(s32[1]{0:T(128)S(6)} %copy.5.profile_ref, f32[3,1,32,1024]{3,2,1,0:T(8,128)} %velocity_ref.1, bf16[2,1024,1024]{2,1,0:T(8,128)(2,1)} %x_hbm.1, bf16[1024,1024]{1,0:T(8,128)(2,1)} %z_hbm.1), custom_call_target="tpu_custom_call" | custom-call | tf_op jit(solution)/shard_map/subgrid/pallas_call | solution.py:434
  46.3 1.0 %sub.3 = f32[6,1,32,1024]{3,2,1,0:T(8,128)} subtract(f32[6,1,32,1024]{3,2,1,0:T(8,128)S(1)} %get-tuple-element.7, f32[6,1,32,1024]{3,2,1,0:T(8,128)S(1)} %get-tuple-element.8) | non-fusion elementwise | flops 196608 | bytes 2359296 | tf_op jit(solution)/shard_map/sub | solution.py:475

commit v4 on v3

--- a/solution.py
+++ b/solution.py
@@ -36,10 +36,10 @@
 
 def kernel(
     sizes,
-    profile_ref, velocity_ref, x_hbm, z_hbm, direct_ref, product_ref,
+    profile_hbm, velocity_ref, x_hbm, z_hbm, direct_ref, product_ref,
     spread, coded, gathered, wide, first, second, advanced, fields, last_low,
     x_mat, z_mat, send_first, send_second, recv_first, recv_second, z_pass,
-    weight_sem, gather_send, gather_recv, profile_sem, local_sem, pass_send, pass_recv, word,
+    weight_sem, gather_send, gather_recv, profile_sem, local_sem, pass_send, pass_recv, word, profile_word,
 ):
     n_grp, n_row, n_col = sizes
     n_blk, n_pln = n_grp * n_row, n_col // 2
@@ -78,10 +78,8 @@
         say(device(blk, pln + 2, 0))
 
     around = [(grp, lax.rem(row + step, n_row), col) for step in (1, n_row - 1)]
-    across = [
-        (grp, row, pln * 2 + other),
-        (grp + 1 - 2 * lax.rem(grp, 2), row, col),
-        (lax.rem(grp + 2, n_grp), row, col),
+    across = [(grp, row, pln * 2 + other)] + [
+        (lax.rem(grp + step, n_grp), row, pln * 2 + side) for step in range(1, n_grp) for side in (0, 1)
     ]
     for target in around + across:
         say(target)
@@ -90,6 +88,8 @@
 
     x_copy = pltpu.make_async_copy(x_hbm, x_mat, weight_sem.at[0])
     z_copy = pltpu.make_async_copy(z_hbm, z_mat, weight_sem.at[1])
+    profile_copy = pltpu.make_async_copy(profile_hbm, profile_word, weight_sem.at[2])
+    profile_copy.start()
     x_copy.start()
     z_copy.start()
 
@@ -108,11 +108,12 @@
         return carry
 
     lax.fori_loop(0, 2 * HALF // 4, encode_cells, 0)
-    own_profile = jnp.full((8, 128), profile_ref[0], jnp.int32)
+    profile_copy.wait()
+    own_profile = jnp.full((8, 128), profile_word[0], jnp.int32)
     for comp in range(3):
         coded[2 * HALF, comp] = own_profile.astype(jnp.int16)
 
-    partners = 7
+    partners = len(across) + len(around) + 2
     for step, count in ((toward, 4), (-toward, 4), (2 * toward, 2)):
         partners = partners + jnp.where(there(pln + step), count, 0)
     pl.semaphore_wait(barrier, partners)
@@ -192,13 +193,15 @@
     def tell(target, turn):
         pl.semaphore_signal(word.at[turn], inc=1, device_id=target, device_id_type=MESH)
 
-    for turn in range(n_row // 2):
-        for target in around:
+    def tell_all(turn):
+        for target in around if turn else across:
             tell(target, turn)
-        pl.semaphore_wait(word.at[turn], 2)
-    for turn, target in enumerate(across):
-        tell(target, n_row // 2 + turn)
-        pl.semaphore_wait(word.at[n_row // 2 + turn], 1)
+
+    def hear_all(turn):
+        pl.semaphore_wait(word.at[turn], len(around if turn else across))
+
+    turns = n_row // 2 + 1
+    tell_all(0)
 
     def arrive(part, line, low, count):
         pltpu.make_async_copy(
@@ -360,11 +363,17 @@
                 pl.when(half == part)(
                     functools.partial(arrive, part, own_line, (0, DEPTH + HALF)[part], DEPTH)
                 )
+                if part == 0:
+                    hear_all(0)
+                    tell_all(1)
                 continue
             for line in (DEPTH - d, DEPTH + 1 + d):
                 pl.when(present[line])(
                     functools.partial(arrive, part, line, (d, 14 - d)[part], (14 - 2 * d, PART)[part])
                 )
+            if part == 0:
+                hear_all(d)
+                tell_all(d + 1)
             for number in range(1, d + 1):
                 sweep(number, part, d - number)
         if part == 0:
@@ -376,6 +385,10 @@
             odd = jnp.where(half == 0, pair_profile, own_profile).astype(F32)
             one = jnp.concatenate([even, odd], axis=0)
             x_copy.wait()
+            for turn in range(4, turns - 1):
+                hear_all(turn)
+                tell_all(turn + 1)
+            hear_all(turns - 1)
         stays.append(pass_part(part, one, 1.0 - one))
     z_copy.wait()
 
@@ -435,7 +448,7 @@
             functools.partial(kernel, sizes),
             out_shape=(result, result),
             in_specs=[
-                pl.BlockSpec(memory_space=pltpu.SMEM),
+                pl.BlockSpec(memory_space=pl.ANY),
                 vmem,
                 pl.BlockSpec(memory_space=pl.ANY),
                 pl.BlockSpec(memory_space=pl.ANY),
@@ -458,14 +471,15 @@
                 pltpu.VMEM((2 * n_blk, 2) + tile, BF16),
                 pltpu.VMEM((2 * n_blk, 3) + tile, BF16),
                 pltpu.VMEM((384, 1024), F32),
-                pltpu.SemaphoreType.DMA((2,)),
+                pltpu.SemaphoreType.DMA((3,)),
                 pltpu.SemaphoreType.DMA((5,)),
                 pltpu.SemaphoreType.DMA((2, ROWS)),
                 pltpu.SemaphoreType.DMA,
                 pltpu.SemaphoreType.DMA((2,)),
                 pltpu.SemaphoreType.DMA((2,)),
                 pltpu.SemaphoreType.DMA((2,)),
-                pltpu.SemaphoreType.REGULAR((sizes[1] // 2 + 3,)),
+                pltpu.SemaphoreType.REGULAR((sizes[1] // 2 + 1,)),
+                pltpu.SMEM((1,), jnp.int32),
             ],
             compiler_params=pltpu.CompilerParams(
                 collective_id=0, has_side_effects=True, vmem_limit_bytes=60000 * 1024

time: 47.4 us -> 47.7 us (level)
  the two profiles are of different devices: /device:TPU:1 before, /device:TPU:129 now
where the time goes in v4:
time: 47.7 us; the launch traced here: 47.5 us
  Pallas kernels  45.9 us (96%)
  other arithmetic  1 us (2%)
  between operations  0.66 us (1%)
    pallas_call x1, Pallas kernels, body(): pl.pallas_call(functools.partial(kernel, sizes), out_shape=(result, resul...  45.9 us
    sub x1, other arithmetic, body(): return direct - product  1 us

profile of v4, /device:TPU:129, one launch (start us, length us, event | category | flops | bytes accessed | tf_op | source)
XLA Modules:
  0.0 47.5 jit_solution(11968751856248681436)
XLA Ops:
  0.7 45.9 %subgrid.1 = (f32[6,1,32,1024]{3,2,1,0:T(8,128)S(1)}, f32[6,1,32,1024]{3,2,1,0:T(8,128)S(1)}) custom-call(s32[1]{0:T(128)S(6)} %copy.5.profile_hbm, f32[3,1,32,1024]{3,2,1,0:T(8,128)} %velocity_ref.1, bf16[2,1024,1024]{2,1,0:T(8,128)(2,1)} %x_hbm.1, bf16[1024,1024]{1,0:T(8,128)(2,1)} %z_hbm.1), custom_call_target="tpu_custom_call" | custom-call | tf_op jit(solution)/shard_map/subgrid/pallas_call | solution.py:447
  46.5 1.0 %sub.3 = f32[6,1,32,1024]{3,2,1,0:T(8,128)} subtract(f32[6,1,32,1024]{3,2,1,0:T(8,128)S(1)} %get-tuple-element.7, f32[6,1,32,1024]{3,2,1,0:T(8,128)S(1)} %get-tuple-element.8) | non-fusion elementwise | flops 196608 | bytes 2359296 | tf_op jit(solution)/shard_map/sub | solution.py:489

commit v5 on v2

--- a/solution.py
+++ b/solution.py
@@ -38,7 +38,7 @@
     sizes,
     profile_ref, velocity_ref, x_hbm, z_hbm, direct_ref, product_ref,
     spread, coded, gathered, wide, first, second, advanced, fields, last_low,
-    x_mat, z_mat, send_first, send_second, recv_first, recv_second, z_pass,
+    x_mat, z_mat, send_first, send_second, recv_first, recv_second, z_pass, order, z_turned,
     weight_sem, gather_send, gather_recv, profile_sem, local_sem, pass_send, pass_recv,
 ):
     n_grp, n_row, n_col = sizes
@@ -186,6 +186,30 @@
         return carry
 
     lax.fori_loop(0, HALF + DEPTH, keep, 0)
+
+    length = 2 * n_blk * HALF
+
+    def reorder(step, carry):
+        start = pl.multiple_of(step * 128, 128)
+        place = lax.broadcasted_iota(jnp.int32, (128, length), 0) + start
+        within = lax.rem(place, length // 2)
+        cell = (within // PART) * HALF + (place // (length // 2)) * PART + lax.rem(within, PART)
+        hit = cell == lax.broadcasted_iota(jnp.int32, (128, length), 1)
+        order[pl.ds(start, 128), :] = jnp.where(hit, 1.0, 0.0).astype(BF16)
+        return carry
+
+    lax.fori_loop(0, length // 128, reorder, 0)
+    z_copy.wait()
+
+    def turn_z(step, carry):
+        start = pl.multiple_of(step * 256, 256)
+        z_turned[:, pl.ds(start, 256)] = lax.dot_general(
+            order[...], z_mat[pl.ds(start, 256), :], (((1,), (1,)), ((), ())),
+            preferred_element_type=F32,
+        ).astype(BF16)
+        return carry
+
+    lax.fori_loop(0, 4, turn_z, 0)
 
     def arrive(part, line, low, count):
         pltpu.make_async_copy(
@@ -364,27 +388,33 @@
             one = jnp.concatenate([even, odd], axis=0)
             x_copy.wait()
         stays.append(pass_part(part, one, 1.0 - one))
-    z_copy.wait()
-
-    contract = (((0,), (1,)), ((), ()))
+
+    contract = (((0,), (0,)), ((), ()))
     many = 2 * n_blk - 1
+    middle = length // 2
+
+    def z_filter(cells, rows):
+        return lax.dot_general(
+            cells.reshape(cells.shape[0] * PART, 128).astype(BF16), z_turned[rows, :], contract,
+            preferred_element_type=F32,
+        )
+
     for part, ref in ((0, recv_first), (1, recv_second)):
         stays[part].wait()
         pltpu.make_async_copy(
             ref.at[pl.ds(0, many)], ref.at[pl.ds(0, many)], pass_recv.at[part]
         ).wait()
-
-    def z_filter(number, low, high):
-        cells = jnp.concatenate([low, high], axis=1).reshape(2 * n_blk * HALF, 128).astype(BF16)
-        z_pass[number * 128:(number + 1) * 128, :] = lax.dot_general(
-            cells, z_mat[...], contract, preferred_element_type=F32
-        )
-
-    for four in range(2):
-        z_filter(four, recv_first[:, four].astype(F32), recv_second[:, four].astype(F32))
+        rows = slice(part * middle, (part + 1) * middle)
+        for four in range(2):
+            filtered_part = z_filter(ref[:, four].astype(F32), rows)
+            lines = slice(four * 128, (four + 1) * 128)
+            if part == 0:
+                z_pass[lines, :] = filtered_part
+            else:
+                z_pass[lines, :] = z_pass[lines, :] + filtered_part
     low = recv_second[:, 2].astype(F32)
     high = pltpu.roll(low.reshape(2 * n_blk * PART, 128), 96, 1).reshape(2 * n_blk, PART, 128)
-    z_filter(2, low, high)
+    z_pass[256:384, :] = z_filter(jnp.concatenate([low, high], axis=0), slice(0, length))
 
     turn = lax.rem(row, 4)
 
@@ -417,7 +447,7 @@
 
     def body(velocity, profile, x_filters, z_filter):
         vmem = pl.BlockSpec(memory_space=pltpu.VMEM)
-        result = jax.ShapeDtypeStruct((6, 1, 32, 1024), F32)
+        result = pltpu.VMEM((6, 1, 32, 1024), F32)
         direct, product = pl.pallas_call(
             functools.partial(kernel, sizes),
             out_shape=(result, result),
@@ -445,6 +475,8 @@
                 pltpu.VMEM((2 * n_blk, 2) + tile, BF16),
                 pltpu.VMEM((2 * n_blk, 3) + tile, BF16),
                 pltpu.VMEM((384, 1024), F32),
+                pltpu.VMEM((1024, 1024), BF16),
+                pltpu.VMEM((1024, 1024), BF16),
                 pltpu.SemaphoreType.DMA((2,)),
                 pltpu.SemaphoreType.DMA((5,)),
                 pltpu.SemaphoreType.DMA((2, ROWS)),

time: 48.5 us -> 44.6 us (0.920)
  Pallas kernels: 45 us -> 42.4 us
  other arithmetic: 2.37 us -> 1 us
    pallas_call x1, Pallas kernels: 45 us -> 42.4 us  [body(): pl.pallas_call(functools.partial(kernel, sizes), out_shape=(result, resul...]
    sub x1, other arithmetic: 2.37 us -> 1 us  [body(): return direct - product]
where the time goes in v5:
time: 44.6 us; the launch traced here: 44.1 us
  Pallas kernels  42.4 us (95%)
  other arithmetic  1 us (2%)
  between operations  0.66 us (1%)
    pallas_call x1, Pallas kernels, body(): pl.pallas_call(functools.partial(kernel, sizes), out_shape=(result, resul...  42.4 us
    sub x1, other arithmetic, body(): return direct - product  1 us

profile of v5, /device:TPU:1, one launch (start us, length us, event | category | flops | bytes accessed | tf_op | source)
XLA Modules:
  0.0 44.1 jit_solution(1816401530314833135)
XLA Ops:
  0.7 42.4 %subgrid.1 = (f32[6,1,32,1024]{3,2,1,0:T(8,128)S(1)}, f32[6,1,32,1024]{3,2,1,0:T(8,128)S(1)}) custom-call(s32[1]{0:T(128)S(6)} %copy.5.profile_ref, f32[3,1,32,1024]{3,2,1,0:T(8,128)} %velocity_ref.1, bf16[2,1024,1024]{2,1,0:T(8,128)(2,1)} %x_hbm.1, bf16[1024,1024]{1,0:T(8,128)(2,1)} %z_hbm.1), custom_call_target="tpu_custom_call" | custom-call | tf_op jit(solution)/shard_map/subgrid/pallas_call | solution.py:451
  43.1 1.0 %sub.3 = f32[6,1,32,1024]{3,2,1,0:T(8,128)} subtract(f32[6,1,32,1024]{3,2,1,0:T(8,128)S(1)} %get-tuple-element.7, f32[6,1,32,1024]{3,2,1,0:T(8,128)S(1)} %get-tuple-element.8) | non-fusion elementwise | flops 196608 | bytes 2359296 | tf_op jit(solution)/shard_map/sub | solution.py:493

commit v6 on v5

--- a/solution.py
+++ b/solution.py
@@ -52,39 +52,50 @@
     def there(plane):
         return (plane >= 0) & (plane < n_pln)
 
+    grps = [grp] + [
+        jnp.where(grp + step < n_grp, grp + step, grp + step - n_grp) for step in range(1, n_grp)
+    ]
+    rows = [row] + [
+        jnp.where(row + step < n_row, row + step, row + step - n_row) for step in range(1, n_row)
+    ]
+    blocks = {
+        0: (grp, row),
+        1: (jnp.where(row == n_row - 1, grps[1], grp), rows[1]),
+        -1: (jnp.where(row == 0, grps[-1], grp), rows[-1]),
+    }
+    beside = tuple(
+        jnp.where(half == 1, after, before) for before, after in zip(blocks[-1], blocks[1])
+    )
+    far_first = (4, 3, 5, 2, 6, 1, 7, 0)
+
     def device(block, plane, side):
-        block = lax.rem(block + n_blk, n_blk)
-        return (block // n_row, lax.rem(block, n_row), plane * 2 + side)
+        return block + (plane * 2 + side,)
 
     barrier = pltpu.get_barrier_semaphore()
 
     def say(target):
         pl.semaphore_signal(barrier, inc=1, device_id=target, device_id_type=MESH)
 
-    beside = blk + toward
+    for off in far_first:
+        for step in range(n_grp):
+            for side in (0, 1):
+                if off or step:
+                    say((grps[step], rows[off], 2 * pln + side))
+    say(device(blocks[0], pln, other))
     for step in (-1, 1):
         @pl.when(there(pln + step))
         def _(step=step):
             for side in (0, 1):
-                say(device(blk, pln + step, side))
+                say(device(blocks[0], pln + step, side))
                 say(device(beside, pln + step, side))
 
     @pl.when(there(pln - 2))
     def _():
-        say(device(blk, pln - 2, 1))
+        say(device(blocks[0], pln - 2, 1))
 
     @pl.when(there(pln + 2))
     def _():
-        say(device(blk, pln + 2, 0))
-
-    say(device(blk, pln, other))
-
-    def say_block(step, carry):
-        say(device(blk + step, pln, 0))
-        say(device(blk + step, pln, 1))
-        return carry
-
-    lax.fori_loop(1, n_blk, say_block, 0)
+        say(device(blocks[0], pln + 2, 0))
 
     x_copy = pltpu.make_async_copy(x_hbm, x_mat, weight_sem.at[0])
     z_copy = pltpu.make_async_copy(z_hbm, z_mat, weight_sem.at[1])
@@ -126,7 +137,7 @@
     pltpu.make_async_remote_copy(
         src_ref=coded.at[pl.ds(2 * HALF, 1)], dst_ref=gathered.at[pl.ds(CELLS, 1)],
         send_sem=gather_send.at[4], recv_sem=profile_sem,
-        device_id=device(blk, pln, other), device_id_type=MESH,
+        device_id=device(blocks[0], pln, other), device_id_type=MESH,
     ).start()
 
     own_line = DEPTH + half
@@ -135,7 +146,7 @@
     for part in range(2):
         for d in range(4):
             def main(side, d=d, part=part):
-                target = device(blk, pln + steps[d], side)
+                target = device(blocks[0], pln + steps[d], side)
                 if part == 0 and side == 0:
                     give(0, 11 - d, DEPTH, part, lines[d], d, target)
                 elif part == 0:
@@ -149,9 +160,9 @@
                 if d == 3:
                     return
                 if part == 0:
-                    give(29 + d, 3 - d, d, part, lines[d], d, device(blk + 1, pln + steps[d], 0))
+                    give(29 + d, 3 - d, d, part, lines[d], d, device(blocks[1], pln + steps[d], 0))
                 else:
-                    give(0, 3 - d, DEPTH + HALF, part, lines[d], d, device(blk - 1, pln + steps[d], 1))
+                    give(0, 3 - d, DEPTH + HALF, part, lines[d], d, device(blocks[-1], pln + steps[d], 1))
 
             if d == 0:
                 for side in (0, 1):
@@ -292,9 +303,9 @@
             ]
             for number, factors in enumerate(FIELD_FACTORS):
                 field = functools.reduce(lambda a, b: a * b, [comps[f] for f in factors])
-                rows = slice(number * 2 * PART, (number + 1) * 2 * PART)
-                fields[rows, chunk * 128:(chunk + 1) * 128] = (field * zero).astype(BF16)
-                fields[rows, 1024 + chunk * 128:1024 + (chunk + 1) * 128] = (field * one).astype(BF16)
+                lines = slice(number * 2 * PART, (number + 1) * 2 * PART)
+                fields[lines, chunk * 128:(chunk + 1) * 128] = (field * zero).astype(BF16)
+                fields[lines, 1024 + chunk * 128:1024 + (chunk + 1) * 128] = (field * one).astype(BF16)
         send_ref = (send_first, send_second)[part]
         recv_ref = (recv_first, recv_second)[part]
 
@@ -329,16 +340,16 @@
                         send_ref[n_blk + dest, four] = mixed[PART:2 * PART].astype(BF16)
                 if part == 1:
                     for line in range(2):
-                        rows = slice(line * PART, (line + 1) * PART)
-                        high = pltpu.roll(passed[128:144, lanes][rows], 32, 1)
-                        low = lows[rows, lanes]
+                        band = slice(line * PART, (line + 1) * PART)
+                        high = pltpu.roll(passed[128:144, lanes][band], 32, 1)
+                        low = lows[band, lanes]
                         for place in range(4):
                             dest = dest_grp * n_row + tile * 4 + place
                             send_ref[line * n_blk + dest, 2] = jnp.where(
                                 small_quarter == place, low, high
                             ).astype(BF16)
-            for off in (4, 3, 5, 2, 6, 1, 7, 0):
-                dest_row = lax.rem(row + off, n_row)
+            for off in far_first:
+                dest_row = rows[off]
                 dest = dest_grp * n_row + dest_row
                 for line in range(2):
                     target = (dest_grp, dest_row, 2 * pln + line)
@@ -404,9 +415,9 @@
         pltpu.make_async_copy(
             ref.at[pl.ds(0, many)], ref.at[pl.ds(0, many)], pass_recv.at[part]
         ).wait()
-        rows = slice(part * middle, (part + 1) * middle)
+        cells = slice(part * middle, (part + 1) * middle)
         for four in range(2):
-            filtered_part = z_filter(ref[:, four].astype(F32), rows)
+            filtered_part = z_filter(ref[:, four].astype(F32), cells)
             lines = slice(four * 128, (four + 1) * 128)
             if part == 0:
                 z_pass[lines, :] = filtered_part

time: 44.6 us -> 44.2 us (level)
  no operation moved by 1% of the time
where the time goes in v6:
time: 44.2 us; the launch traced here: 44 us
  Pallas kernels  42.4 us (96%)
  other arithmetic  1 us (2%)
  between operations  0.66 us (1%)
    pallas_call x1, Pallas kernels, body(): pl.pallas_call(functools.partial(kernel, sizes), out_shape=(result, resul...  42.4 us
    sub x1, other arithmetic, body(): return direct - product  1 us

profile of v6, /device:TPU:1, one launch (start us, length us, event | category | flops | bytes accessed | tf_op | source)
XLA Modules:
  0.0 44.0 jit_solution(6019386138126709998)
XLA Ops:
  0.7 42.4 %subgrid.1 = (f32[6,1,32,1024]{3,2,1,0:T(8,128)S(1)}, f32[6,1,32,1024]{3,2,1,0:T(8,128)S(1)}) custom-call(s32[1]{0:T(128)S(6)} %copy.5.profile_ref, f32[3,1,32,1024]{3,2,1,0:T(8,128)} %velocity_ref.1, bf16[2,1024,1024]{2,1,0:T(8,128)(2,1)} %x_hbm.1, bf16[1024,1024]{1,0:T(8,128)(2,1)} %z_hbm.1), custom_call_target="tpu_custom_call" | custom-call | tf_op jit(solution)/shard_map/subgrid/pallas_call | solution.py:462
  43.0 1.0 %sub.3 = f32[6,1,32,1024]{3,2,1,0:T(8,128)} subtract(f32[6,1,32,1024]{3,2,1,0:T(8,128)S(1)} %get-tuple-element.7, f32[6,1,32,1024]{3,2,1,0:T(8,128)S(1)} %get-tuple-element.8) | non-fusion elementwise | flops 196608 | bytes 2359296 | tf_op jit(solution)/shard_map/sub | solution.py:504

commit v7 on v6

--- a/solution.py
+++ b/solution.py
@@ -226,7 +226,7 @@
         pltpu.make_async_copy(
             gathered.at[pl.ds(0, count)], gathered.at[pl.ds(0, count)], gather_recv.at[part, line]
         ).wait()
-        per = 2 if count % 2 == 0 else 1
+        per = count // 2 if count % 2 == 0 else count
 
         def some(step, carry):
             for cell in range(per):
@@ -271,11 +271,13 @@
         scale, old = ((1.0, None), (0.25, 0.75), (2.0 / 3.0, 1.0 / 3.0))[number - 1]
         low, high = ((d + number, 14 - d - number), (14 - d - number, 22 - d - number))[part]
 
-        def two(step, carry):
+        per = 5 if (high - low) % 4 else 4
+
+        def some(step, carry):
             done = []
             for line in (DEPTH - d, DEPTH + 1 + d):
-                for cell in range(2):
-                    place = low + 2 * step + cell
+                for cell in range(per):
+                    place = low + per * step + cell
                     done.append((line, place, advance(source, scale, old, line * WIDE + place)))
             for line, place, results in done:
                 for comp in range(3):
@@ -289,7 +291,7 @@
                     (first, second)[number - 1][line * WIDE + place, comp] = value
             return carry
 
-        lax.fori_loop(0, (high - low) // 2, two, 0)
+        lax.fori_loop(0, (high - low) // per, some, 0)
 
     wide_lane = lax.broadcasted_iota(jnp.int32, (2 * PART, 128), 1)
     quarter = wide_lane // 32

time: 44.2 us -> 43.3 us (0.980)
  the two profiles are of different devices: /device:TPU:1 before, /device:TPU:128 now
where the time goes in v7:
time: 43.3 us; the launch traced here: 43.1 us
  Pallas kernels  41.5 us (96%)
  other arithmetic  1 us (2%)
  between operations  0.66 us (2%)
    pallas_call x1, Pallas kernels, body(): pl.pallas_call(functools.partial(kernel, sizes), out_shape=(result, resul...  41.5 us
    sub x1, other arithmetic, body(): return direct - product  1 us

profile of v7, /device:TPU:128, one launch (start us, length us, event | category | flops | bytes accessed | tf_op | source)
XLA Modules:
  0.0 43.1 jit_solution(11954244211986307796)
XLA Ops:
  0.7 41.5 %subgrid.1 = (f32[6,1,32,1024]{3,2,1,0:T(8,128)S(1)}, f32[6,1,32,1024]{3,2,1,0:T(8,128)S(1)}) custom-call(s32[1]{0:T(128)S(6)} %copy.5.profile_ref, f32[3,1,32,1024]{3,2,1,0:T(8,128)} %velocity_ref.1, bf16[2,1024,1024]{2,1,0:T(8,128)(2,1)} %x_hbm.1, bf16[1024,1024]{1,0:T(8,128)(2,1)} %z_hbm.1), custom_call_target="tpu_custom_call" | custom-call | tf_op jit(solution)/shard_map/subgrid/pallas_call | solution.py:464
  42.1 1.0 %sub.3 = f32[6,1,32,1024]{3,2,1,0:T(8,128)} subtract(f32[6,1,32,1024]{3,2,1,0:T(8,128)S(1)} %get-tuple-element.7, f32[6,1,32,1024]{3,2,1,0:T(8,128)S(1)} %get-tuple-element.8) | non-fusion elementwise | flops 196608 | bytes 2359296 | tf_op jit(solution)/shard_map/sub | solution.py:506

commit v8 on v7

--- a/solution.py
+++ b/solution.py
@@ -271,7 +271,7 @@
         scale, old = ((1.0, None), (0.25, 0.75), (2.0 / 3.0, 1.0 / 3.0))[number - 1]
         low, high = ((d + number, 14 - d - number), (14 - d - number, 22 - d - number))[part]
 
-        per = 5 if (high - low) % 4 else 4
+        per = {12: 6, 10: 5, 8: 8}[high - low]
 
         def some(step, carry):
             done = []

time: 43.3 us -> 43 us (level)
  the two profiles are of different devices: /device:TPU:128 before, /device:TPU:1 now
where the time goes in v8:
time: 43 us; the launch traced here: 42.5 us
  Pallas kernels  40.9 us (95%)
  other arithmetic  1 us (2%)
  between operations  0.66 us (2%)
    pallas_call x1, Pallas kernels, body(): pl.pallas_call(functools.partial(kernel, sizes), out_shape=(result, resul...  40.9 us
    sub x1, other arithmetic, body(): return direct - product  1 us

profile of v8, /device:TPU:1, one launch (start us, length us, event | category | flops | bytes accessed | tf_op | source)
XLA Modules:
  0.0 42.5 jit_solution(11200229679151576989)
XLA Ops:
  0.7 40.9 %subgrid.1 = (f32[6,1,32,1024]{3,2,1,0:T(8,128)S(1)}, f32[6,1,32,1024]{3,2,1,0:T(8,128)S(1)}) custom-call(s32[1]{0:T(128)S(6)} %copy.5.profile_ref, f32[3,1,32,1024]{3,2,1,0:T(8,128)} %velocity_ref.1, bf16[2,1024,1024]{2,1,0:T(8,128)(2,1)} %x_hbm.1, bf16[1024,1024]{1,0:T(8,128)(2,1)} %z_hbm.1), custom_call_target="tpu_custom_call" | custom-call | tf_op jit(solution)/shard_map/subgrid/pallas_call | solution.py:464
  41.5 1.0 %sub.3 = f32[6,1,32,1024]{3,2,1,0:T(8,128)} subtract(f32[6,1,32,1024]{3,2,1,0:T(8,128)S(1)} %get-tuple-element.7, f32[6,1,32,1024]{3,2,1,0:T(8,128)S(1)} %get-tuple-element.8) | non-fusion elementwise | flops 196608 | bytes 2359296 | tf_op jit(solution)/shard_map/sub | solution.py:506
